TPU v7x, 128 devices: a whole 4x4x4 slice. The times are simulated.
128 devices in a mesh: seq: 32 (over y, z, core), head: 4 (over x).
Axes of the slice: x: 4, y: 4, z: 4, core: 2. Of those that a mesh axis runs over, the one named last changes fastest.
Arguments:
- hidden: bfloat16 [16384, 4096], P('seq'), may hold values from -6 to 6
- positions: int32 [16384], P('seq'), may hold values from 0 to 3342335, as said below
- w_x: bfloat16 [4096, 4096], P('seq', 'head'), may hold values from -0.09375 to 0.09375
- w_bc: bfloat16 [4096, 1024], P('seq', 'head'), may hold values from -0.0078125 to 0.0078125
- w_dt: bfloat16 [4096, 64], P('seq', 'head'), may hold values from -0.09375 to 0.09375
- a_log: float32 [64], P('head'), may hold values from -10 to -4
- dt_bias: float32 [64], P('head'), may hold values from -1 to 1
- d_skip: float32 [64], P('head'), may hold values from 0.5 to 1.5
- grad_out: bfloat16 [16384, 4096], P('seq', 'head'), may hold values from -6 to 6
Outputs:
- d_hidden: bfloat16 [16384, 4096], P('seq', 'head')
- d_w_x: bfloat16 [4096, 4096], P('seq', 'head')
- d_w_bc: bfloat16 [4096, 1024], P('seq', 'head')
- d_w_dt: bfloat16 [4096, 64], P('seq', 'head')
- d_head_params: float32 [3, 64], P(None, 'head')
Inputs may be any that keep to these rules, and one draw needn't show every extreme that they name: positions rise strictly from token to token.
All inputs are finite; a program needn't handle non-finite values.
Results may differ from a plain program's by a relative error of at most 0.034.
Values may be sent and summed in bfloat16 or wider, within the bound.
A program may use at most 192 MiB of HBM per device.

v0:
```python
import functools

import jax
import jax.numpy as jnp
from jax import lax
from jax.experimental import pallas as pl
from jax.experimental.pallas import tpu as pltpu
from jax.sharding import PartitionSpec as P

STATE = 128
HEAD_DIM = 64
TILE = 256
LOG2E = 1.4426950408889634
MESH = pl.DeviceIdType.MESH
F32 = jnp.float32
BF16 = jnp.bfloat16
EXACT = lax.Precision.HIGHEST


def dot(a, b, dims, precision=None):
    return lax.dot_general(a, b, (dims, ((), ())), precision=precision, preferred_element_type=F32)


NN = ((1,), (0,))
NT = ((1,), (1,))
TN = ((0,), (0,))


def split2(v):
    hi = v.astype(BF16)
    return hi, (v - hi.astype(F32)).astype(BF16)


def split3(v):
    hi = v.astype(BF16)
    rest = v - hi.astype(F32)
    mid = rest.astype(BF16)
    return hi, mid, (rest - mid.astype(F32)).astype(BF16)


def spread(v, pick):
    parts = split3(v)
    return dot(jnp.concatenate(parts, axis=0), jnp.concatenate([pick] * 3, axis=0), TN)


def gather_heads(pick, y):
    hi, lo = split2(y)
    return dot(pick, hi, NT) + dot(pick, lo, NT)


def picker(heads, width):
    row = lax.broadcasted_iota(jnp.int32, (heads, heads * width), 0)
    col = lax.broadcasted_iota(jnp.int32, (heads, heads * width), 1)
    return jnp.where(col // width == row, 1.0, 0.0).astype(BF16)


def sigmoid(v):
    return 1.0 / (1.0 + jnp.exp(-v))


def scan_kernel(
    n,
    xp_ref,
    bc_ref,
    dtp_ref,
    gap_ref,
    rate_ref,
    skip_ref,
    g_ref,
    gcols_ref,
    gdt_ref,
    sums_ref,
    pay,
    got,
    back,
    home,
    decs,
    xs_ref,
    tail_ref,
    dtx_ref,
    xd_ref,
    xt_ref,
    ge_ref,
    u_ref,
    colb_ref,
    cumt_ref,
    cbt_ref,
    dcbt_ref,
    rowe_ref,
    cole_ref,
    send1,
    recv1,
    send2,
    recv2,
):
    tokens, width = xp_ref.shape
    heads = dtp_ref.shape[0]
    blocks = tokens // TILE
    piece = width // n
    me = lax.axis_index("seq")

    barrier = pltpu.get_barrier_semaphore()

    def greet(k, carry):
        pl.semaphore_signal(
            barrier, inc=1, device_id={"seq": lax.rem(me + k, n)}, device_id_type=MESH
        )
        return carry

    lax.fori_loop(1, n, greet, 0)

    pick = picker(heads, HEAD_DIM)
    dtp = dtp_ref[...]
    dt = jnp.maximum(dtp, 0.0) + jnp.log1p(jnp.exp(-jnp.abs(dtp)))
    rate = rate_ref[...]
    gap = gap_ref[...]
    decay = -rate * dt * gap
    before = lax.broadcasted_iota(jnp.int32, (tokens, tokens), 0)
    after = lax.broadcasted_iota(jnp.int32, (tokens, tokens), 1)
    upto = jnp.where(before <= after, 1.0, 0.0).astype(BF16)
    parts = jnp.concatenate(split3(decay * LOG2E), axis=0)
    raw = dot(parts, upto, NN)
    cum = raw[:heads] + raw[heads : 2 * heads] + raw[2 * heads :]
    cumt_ref[...] = cum
    last = cum[:, tokens - 1 :]
    whole = jnp.exp2(last)
    ecum = jnp.exp2(cum)
    tail = jnp.exp2(last - cum)

    colb_ref[...] = spread(cum, picker(heads, 128))
    dtx_ref[...] = spread(dt, pick)
    tail_ref[...] = spread(tail, pick)
    sums_skip = jnp.zeros((heads, 1), F32)
    for b in range(blocks):
        rows = pl.ds(b * TILE, TILE)
        xp = xp_ref[rows, :]
        xs = xp * sigmoid(xp)
        xs_ref[rows, :] = xs
        xd = xs * dtx_ref[rows, :]
        xd_ref[rows, :] = xd.astype(BF16)
        xt_ref[rows, :] = (xd * tail_ref[rows, :]).astype(BF16)
        g = g_ref[rows, :].astype(F32)
        ge_ref[rows, :] = (g * spread(ecum[:, b * TILE : (b + 1) * TILE], pick)).astype(BF16)
        sums_skip += jnp.sum(gather_heads(pick, g * xs), axis=1, keepdims=True)
    b_low = bc_ref[:, :STATE].astype(BF16)
    c_low = bc_ref[:, STATE:].astype(BF16)

    parts = split3(jnp.broadcast_to(whole, (heads, STATE)))
    for k in range(3):
        decs[k] = parts[k].astype(F32)
    local_state = dot(xt_ref[...], b_low, TN).astype(BF16)
    local_adjoint = dot(ge_ref[...], c_low, TN).astype(BF16)
    pay[:, :piece, :] = local_state.reshape(n, piece, STATE)
    pay[:, piece : 2 * piece, :] = local_adjoint.reshape(n, piece, STATE)
    which = lax.broadcasted_iota(jnp.int32, (16, STATE), 0)
    per_head = n // heads

    def fill(h, carry):
        one = [jnp.broadcast_to(decs[k, pl.ds(h, 1), :], (16, STATE)) for k in range(3)]
        block = jnp.where(which == 0, one[0], jnp.where(which == 1, one[1], one[2])).astype(BF16)
        for k in range(per_head):
            pay[h * per_head + k, 2 * piece :, :] = block
        return carry

    lax.fori_loop(0, heads, fill, 0)
    got[me] = pay[me]
    pl.semaphore_wait(barrier, n - 1)

    def out_copy(k):
        to = lax.rem(me + k, n)
        return pltpu.make_async_remote_copy(
            pay.at[to], got.at[me], send1.at[k], recv1.at[k], {"seq": to}, MESH
        )

    def start_out(k, carry):
        out_copy(k).start()
        return carry

    lax.fori_loop(1, n, start_out, 0)

    for i in range(blocks):
        for j in range(i, blocks):
            cbt_ref[i, j] = dot(
                b_low[i * TILE : (i + 1) * TILE], c_low[j * TILE : (j + 1) * TILE], NT
            )
            dcbt_ref[i, j] = jnp.zeros((TILE, TILE), F32)
    cole_ref[...] = jnp.zeros_like(cole_ref)
    s_at = lax.broadcasted_iota(jnp.int32, (TILE, TILE), 0)
    t_at = lax.broadcasted_iota(jnp.int32, (TILE, TILE), 1)
    lane = lax.broadcasted_iota(jnp.int32, (TILE, 128), 1)

    def pair(q, carry):
        cols = pl.ds(pl.multiple_of(q * 128, 128), 128)
        rowe = [[jnp.zeros((1, TILE), F32) for _ in range(blocks)] for _ in range(2)]
        for i in range(blocks):
            srows = pl.ds(i * TILE, TILE)
            xd = xd_ref[srows, cols]
            us = []
            for side in range(2):
                h = q * 2 + side
                lanes = slice(side * HEAD_DIM, (side + 1) * HEAD_DIM)
                col = colb_ref[srows, pl.ds(pl.multiple_of(h * 128, 128), 128)]
                col = jnp.concatenate([col] * (TILE // 128), axis=1)
                u = jnp.zeros((TILE, HEAD_DIM), F32)
                cole = jnp.zeros((TILE, 1), F32)
                for j in range(i, blocks):
                    g = g_ref[pl.ds(j * TILE, TILE), cols][:, lanes]
                    diff = cumt_ref[pl.ds(h, 1), pl.ds(j * TILE, TILE)] - col
                    if i == j:
                        diff = jnp.where(t_at >= s_at, diff, -jnp.inf)
                    within = jnp.exp2(diff)
                    f = within * dot(xd[:, lanes], g, NT)
                    dcbt_ref[i, j] += f
                    cb = cbt_ref[i, j]
                    e = cb * f
                    rowe[side][j] += jnp.sum(e, axis=0, keepdims=True)
                    cole += jnp.sum(e, axis=1, keepdims=True)
                    u += dot((within * cb).astype(BF16), g, NN)
                us.append(u)
                cole_ref[srows, :] = jnp.where(lane == h, cole, cole_ref[srows, :])
            u_ref[srows, cols] = jnp.concatenate(us, axis=1)
        for side in range(2):
            rowe_ref[pl.ds(q * 2 + side, 1), :] = jnp.concatenate(rowe[side], axis=1)
        return carry

    pairs = heads // 2
    lax.fori_loop(0, pairs // 2, pair, 0)

    def wait_out(k, carry):
        out_copy(k).wait_recv()
        return carry

    lax.fori_loop(1, n, wait_out, 0)

    def decay_of(d):
        rows = got[d, 2 * piece :, :].astype(F32)
        return rows[0:1] + rows[1:2] + rows[2:3]

    def ahead(d, state):
        back[d, :piece, :] = state.astype(BF16)
        return decay_of(d) * state + got[d, :piece, :].astype(F32)

    def behind(k, state):
        d = n - 1 - k
        back[d, piece:, :] = state.astype(BF16)
        return decay_of(d) * state + got[d, piece : 2 * piece, :].astype(F32)

    zero = jnp.zeros((piece, STATE), F32)
    lax.fori_loop(0, n, ahead, zero)
    lax.fori_loop(0, n, behind, zero)
    home[me] = back[me]

    def back_copy(k):
        to = lax.rem(me + k, n)
        return pltpu.make_async_remote_copy(
            back.at[to], home.at[me], send2.at[k], recv2.at[k], {"seq": to}, MESH
        )

    def start_back(k, carry):
        back_copy(k).start()
        return carry

    lax.fori_loop(1, n, start_back, 0)
    lax.fori_loop(pairs // 2, pairs, pair, 0)

    def wait_back(k, carry):
        back_copy(k).wait_recv()
        back_copy(k).wait_send()
        out_copy(k).wait_send()
        return carry

    lax.fori_loop(1, n, wait_back, 0)

    s_in = home[:, :piece, :].reshape(width, STATE)
    d_out = home[:, piece:, :].reshape(width, STATE)
    gcum = rowe_ref[...] - cole_ref[...].T[:heads]
    grad_dt_parts, r_parts, off_parts = [], [], []
    skipx = spread(jnp.broadcast_to(skip_ref[...], (heads, 128)), pick)[0:1]
    for b in range(blocks):
        rows = pl.ds(b * TILE, TILE)
        bb, cc = b_low[b * TILE : (b + 1) * TILE], c_low[b * TILE : (b + 1) * TILE]
        tq = tail_ref[rows, :] * dot(bb, d_out, NT)
        z = u_ref[rows, :] + tq
        xs = xs_ref[rows, :]
        grad_dt_parts.append(gather_heads(pick, xs * z))
        r_parts.append(gather_heads(pick, xs * tq))
        off_parts.append(gather_heads(pick, ge_ref[rows, :].astype(F32) * dot(cc, s_in, NT)))
        grad_x = dtx_ref[rows, :] * z + skipx * g_ref[rows, :].astype(F32)
        xp = xp_ref[rows, :]
        sig = sigmoid(xp)
        gcols_ref[rows, :width] = (grad_x * (sig + xp * sig * (1.0 - sig))).astype(BF16)
        grad_b = dot(xt_ref[rows, :], d_out, NN)
        grad_c = dot(ge_ref[rows, :], s_in, NN)
        for j in range(b, blocks):
            grad_b += dot(
                dcbt_ref[b, j].astype(BF16), c_low[j * TILE : (j + 1) * TILE], NN
            )
        for i in range(b + 1):
            grad_c += dot(
                dcbt_ref[i, b].astype(BF16), b_low[i * TILE : (i + 1) * TILE], TN
            )
        gcols_ref[rows, width : width + STATE] = grad_b.astype(BF16)
        gcols_ref[rows, width + STATE :] = grad_c.astype(BF16)
    grad_dt = jnp.concatenate(grad_dt_parts, axis=1)
    r = dt * jnp.concatenate(r_parts, axis=1)
    gcum += jnp.concatenate(off_parts, axis=1) - r
    both = jnp.sum(s_in.astype(F32) * d_out.astype(F32), axis=1, keepdims=True)
    both = jnp.broadcast_to(both, (width, 128))
    hi, lo = split2(both)
    both = (dot(pick, hi, NN) + dot(pick, lo, NN))[:, :1]
    at_end = jnp.sum(r, axis=1, keepdims=True) + whole * both
    parts = jnp.concatenate(split3(gcum), axis=0)
    raw = dot(parts, upto, NT)
    grad_decay = raw[:heads] + raw[heads : 2 * heads] + raw[2 * heads :] + at_end
    grad_dt_pre = (grad_dt - grad_decay * rate * gap) * sigmoid(dtp)
    gdt_ref[...] = grad_dt_pre.astype(BF16)
    slot = lax.broadcasted_iota(jnp.int32, (heads, 128), 1)
    sum_a = jnp.sum(grad_decay * decay, axis=1, keepdims=True)
    sum_b = jnp.sum(grad_dt_pre, axis=1, keepdims=True)
    sums_ref[...] = jnp.where(slot == 0, sum_a, jnp.where(slot == 1, sum_b, sums_skip))


def scan_call(n, xp, bc, dtp, gap, rate, skip, g):
    tokens, width = xp.shape
    heads = dtp.shape[0]
    blocks = tokens // TILE
    piece = width // n
    vm = pl.BlockSpec(memory_space=pltpu.VMEM)
    return pl.pallas_call(
        functools.partial(scan_kernel, n),
        name="scan",
        out_shape=(
            jax.ShapeDtypeStruct((tokens, width + 2 * STATE), BF16),
            jax.ShapeDtypeStruct((heads, tokens), BF16),
            jax.ShapeDtypeStruct((heads, 128), F32),
        ),
        in_specs=[vm] * 7,
        out_specs=(vm, vm, vm),
        scratch_shapes=[
            pltpu.VMEM((n, 2 * piece + 16, STATE), BF16),
            pltpu.VMEM((n, 2 * piece + 16, STATE), BF16),
            pltpu.VMEM((n, 2 * piece, STATE), BF16),
            pltpu.VMEM((n, 2 * piece, STATE), BF16),
            pltpu.VMEM((3, heads, STATE), F32),
            pltpu.VMEM((tokens, width), F32),
            pltpu.VMEM((tokens, width), F32),
            pltpu.VMEM((tokens, width), F32),
            pltpu.VMEM((tokens, width), BF16),
            pltpu.VMEM((tokens, width), BF16),
            pltpu.VMEM((tokens, width), BF16),
            pltpu.VMEM((tokens, width), F32),
            pltpu.VMEM((tokens, heads * 128), F32),
            pltpu.VMEM((heads, tokens), F32),
            pltpu.VMEM((blocks, blocks, TILE, TILE), F32),
            pltpu.VMEM((blocks, blocks, TILE, TILE), F32),
            pltpu.VMEM((heads, tokens), F32),
            pltpu.VMEM((tokens, 128), F32),
            pltpu.SemaphoreType.DMA((n,)),
            pltpu.SemaphoreType.DMA((n,)),
            pltpu.SemaphoreType.DMA((n,)),
            pltpu.SemaphoreType.DMA((n,)),
        ],
        compiler_params=pltpu.CompilerParams(
            collective_id=1, has_side_effects=True, vmem_limit_bytes=60 * 2**20
        ),
    )(xp, bc, dtp, gap, rate, skip, g)


def total_kernel(n, in_ref, out_ref, got, send, recv):
    me = lax.axis_index("seq")
    barrier = pltpu.get_barrier_semaphore()

    def greet(k, carry):
        pl.semaphore_signal(
            barrier, inc=1, device_id={"seq": lax.rem(me + k, n)}, device_id_type=MESH
        )
        return carry

    lax.fori_loop(1, n, greet, 0)
    pl.semaphore_wait(barrier, n - 1)

    def copy(k):
        to = lax.rem(me + k, n)
        return pltpu.make_async_remote_copy(
            in_ref, got.at[me], send.at[k], recv.at[k], {"seq": to}, MESH
        )

    def start(k, carry):
        copy(k).start()
        return carry

    lax.fori_loop(1, n, start, 0)
    got[me] = in_ref[...]

    def wait(k, carry):
        copy(k).wait()
        return carry

    lax.fori_loop(1, n, wait, 0)
    out_ref[...] = jnp.sum(got[...], axis=0)


def total_call(n, value):
    vm = pl.BlockSpec(memory_space=pltpu.VMEM)
    return pl.pallas_call(
        functools.partial(total_kernel, n),
        name="total",
        out_shape=jax.ShapeDtypeStruct(value.shape, value.dtype),
        in_specs=[vm],
        out_specs=vm,
        scratch_shapes=[
            pltpu.VMEM((n,) + value.shape, value.dtype),
            pltpu.SemaphoreType.DMA((n,)),
            pltpu.SemaphoreType.DMA((n,)),
        ],
        compiler_params=pltpu.CompilerParams(collective_id=2, has_side_effects=True),
    )(value)


def body(n, hidden, positions, w_x, w_bc, w_dt, a_log, dt_bias, d_skip, grad_out):
    inner = w_x.shape[1]
    heads = w_dt.shape[1]
    maps = w_bc.shape[1]
    w_local = jnp.concatenate([w_x, w_bc, w_dt], axis=1)
    w_all = lax.all_gather(w_local, "seq", axis=0, tiled=True)
    projected = jnp.dot(hidden, w_all, preferred_element_type=F32)
    dtp = projected[:, inner + maps :].T + dt_bias[:, None]
    pairs = [(i, i + 1) for i in range(n - 1)]
    earlier = lax.ppermute(positions[-1:], "seq", pairs)
    gap = (positions - jnp.concatenate([earlier, positions[:-1]])).astype(F32)[None, :]
    rate = jnp.exp(a_log)[:, None]
    gcols, gdt, sums = scan_call(
        n,
        projected[:, :inner],
        projected[:, inner : inner + maps],
        dtp,
        gap,
        rate,
        d_skip[:, None],
        grad_out,
    )
    totals = total_call(n, sums)
    d_head_params = totals[:, :3].T
    grad_cols = jnp.concatenate([gcols, gdt.T], axis=1)
    hidden_terms = lax.dot_general(
        grad_cols, w_all, (((1,), (1,)), ((), ())), preferred_element_type=F32
    )
    d_hidden = lax.psum_scatter(
        hidden_terms.astype(BF16), "head", scatter_dimension=1, tiled=True
    )
    weight_grads = lax.psum_scatter(
        lax.dot_general(
            hidden, grad_cols, (((0,), (0,)), ((), ())), preferred_element_type=F32
        ).astype(BF16),
        "seq",
        scatter_dimension=0,
        tiled=True,
    )
    return (
        d_hidden,
        weight_grads[:, :inner],
        weight_grads[:, inner : inner + maps],
        weight_grads[:, inner + maps :],
        d_head_params,
    )


def solution(mesh):
    return jax.shard_map(
        functools.partial(body, mesh.shape["seq"]),
        mesh=mesh,
        in_specs=(
            P("seq", None),
            P("seq"),
            P("seq", "head"),
            P("seq", "head"),
            P("seq", "head"),
            P("head"),
            P("head"),
            P("head"),
            P("seq", "head"),
        ),
        out_specs=(
            P("seq", "head"),
            P("seq", "head"),
            P("seq", "head"),
            P("seq", "head"),
            P(None, "head"),
        ),
        check_vma=False,
    )
```

profile of v0, /device:TPU:1, one launch (start us, length us, event | category | flops | bytes accessed | tf_op | source)
XLA Modules:
  0.0 308.2 jit_solution(1311599914487394021)
XLA Ops:
  7.2 0.0 all-gather.2.cloned.1.call-start
  7.2 0.8 copy.23
  8.0 1.8 pad_maximum_fusion.3
  9.8 0.0 all-gather.2.cloned.1.call-update
  9.8 0.0 reduce-scatter.7.cloned.1.call-start
  9.8 1.3 slice.30
  11.1 4.9 %collective-permute-start = (s32[1]{0:T(128)}, s32[1]{0:T(128)}, u32[]{:S(2)}, u32[]{:S(2)}) collective-permute-start(s32[1]{0:T(128)} %slice.30), channel_id=1, source_target_pairs={{0,4},{4,8},{8,12},{12,16},{16,20},{20,24},{24,28},{28,32},{32,36}... | collective-permute-start | bytes 20 | tf_op jit(solution)/shard_map/ppermute | solution.py:429
  16.0 0.7 exponential_bitcast_fusion
  16.7 0.7 copy.26.rate_ref
  17.4 1.3 copy.27.skip_ref
  18.7 0.0 collective-permute-done
  18.7 2.0 fusion.2
  20.7 54.0 %all-gather.2.cloned.1.call-done = bf16[4096,1296]{1,0:T(8,128)(2,1)} async-done(((bf16[128,1296]{1,0:T(8,128)(2,1)}), bf16[4096,1296]{1,0:T(8,128)(2,1)}) %all-gather.2.cloned.1.call-update) | async-done | bytes 10616848 | tf_op jit(solution)/shard_map/all_gather | solution.py:425
  74.8 12.8 %convolution_bitcast_fusion = f32[512,1296]{0,1:T(8,128)S(1)} fusion(bf16[4096,1296]{1,0:T(8,128)(2,1)} %all-gather.2.cloned.1.call-done, bf16[512,4096]{1,0:T(8,128)(2,1)} %param.9), kind=kOutput, calls=%fused_computation.3 | convolution fusion | flops 5435817984 | bytes 17465344 | tf_op jit(solution)/shard_map/dot_general | solution.py:426
  87.6 0.0 copy-start
  87.6 0.0 copy-start.1
  87.6 0.2 slice.36
  87.8 1.4 copy-done
  89.2 0.0 copy-done.1
  89.2 0.7 fusion.1.dtp_ref
  89.9 0.0 slice-start
  89.9 1.9 copy.24.xp_ref
  91.7 0.0 slice-done
  91.7 1.0 copy.25.bc_ref
  92.7 34.1 %scan.1 = (bf16[512,1280]{1,0:T(8,128)(2,1)}, bf16[16,512]{1,0:T(8,128)(2,1)}, f32[16,128]{1,0:T(8,128)}) custom-call(f32[512,1024]{1,0:T(8,128)} %copy.24.xp_ref, f32[512,256]{1,0:T(8,128)} %copy.25.bc_ref, f32[16,512]{1,0:T(8,128)} %fusion.1.dtp_ref, f32[1,512]{1,0:T(1,128)} %bitcast.20, f32[16,1]{1,0:T(8,128)} %copy.26.rate_ref, f32[16,1]{1,0:T(8,128)} %copy.27.skip_ref, ...), custom_call_target="tpu_custom_call" | custom-call | tf_op jit(solution)/shard_map/scan/pallas_call | solution.py:329
  126.8 0.8 copy.28
  127.6 10.3 %fusion = bf16[4096,1296]{0,1:T(8,128)(2,1)} fusion(bf16[512,4096]{1,0:T(8,128)(2,1)} %param.9, bf16[512,16]{1,0:T(8,128)(2,1)S(1)} %copy.28, bf16[512,1280]{1,0:T(8,128)(2,1)} %get-tuple-element.8), kind=kOutput, calls=%fused_computation.1 | convolution fusion | flops 5443780608 | bytes 16138240 | tf_op jit(solution)/shard_map/dot_general | solution.py:452
  138.0 14.9 %copy.32 = bf16[4096,1296]{1,0:T(8,128)(2,1)} copy(bf16[4096,1296]{0,1:T(8,128)(2,1)} %fusion) | data formatting | bytes 21233664
  152.9 0.0 copy-start.2
  152.9 0.0 reduce-scatter.7.cloned.1.call-update
  152.9 0.0 reduce-scatter.5.cloned.1.call-start
  152.9 1.2 copy-done.2
  154.2 12.5 %convolution_convert_fusion.1 = bf16[512,4096]{1,0:T(8,128)(2,1)} fusion(bf16[4096,1296]{1,0:T(8,128)(2,1)} %all-gather.2.cloned.1.call-done, bf16[512,16]{1,0:T(8,128)(2,1)S(1)} %copy.28, bf16[512,1280]{1,0:T(8,128)(2,1)S(1)} %copy-done.2), kind=kOutput, calls=%fused_computation.2 | convolution fusion | flops 5440569344 | bytes 16138240 | tf_op jit(solution)/shard_map/dot_general | solution.py:445
  166.7 0.0 reduce-scatter.5.cloned.1.call-update
  166.7 11.8 %total.1 = f32[16,128]{1,0:T(8,128)} custom-call(f32[16,128]{1,0:T(8,128)} %get-tuple-element.10.in_ref), custom_call_target="tpu_custom_call" | custom-call | tf_op jit(solution)/shard_map/total/pallas_call | solution.py:405
  178.6 0.7 slice_bitcast_fusion
  179.3 0.7 copy.31
  179.9 71.1 %reduce-scatter.7.cloned.1.call-done = bf16[128,1296]{1,0:T(8,128)(2,1)} async-done(((bf16[4096,1296]{1,0:T(8,128)(2,1)}), bf16[128,1296]{1,0:T(8,128)(2,1)}) %reduce-scatter.7.cloned.1.call-update) | async-done | bytes 331792
  251.0 0.8 slice.41
  251.7 0.7 copy.36
  252.4 1.5 slice.40
  253.9 1.7 slice.39
  255.6 46.1 %reduce-scatter.5.cloned.1.call-done = bf16[512,1024]{1,0:T(8,128)(2,1)} async-done(((bf16[512,4096]{1,0:T(8,128)(2,1)}), bf16[512,1024]{1,0:T(8,128)(2,1)}) %reduce-scatter.5.cloned.1.call-update) | async-done | bytes 1048592 | tf_op jit(solution)/shard_map/reduce_scatter | solution.py:448
Async XLA Ops:
  7.2 67.6 %all-gather.2.cloned.1.call-start = ((), (), s32[]{:S(2)}) async-start(), calls=%async_computation.2 | async-start | bytes 11894784 | tf_op jit(solution)/shard_map/all_gather | solution.py:425
  9.8 241.2 %reduce-scatter.7.cloned.1.call-start = ((), (), s32[]{:S(2)}) async-start(), calls=%async_computation.4 | async-start | bytes 11894784
  11.1 7.6 %collective-permute-start = (s32[1]{0:T(128)}, s32[1]{0:T(128)}, u32[]{:S(2)}, u32[]{:S(2)}) collective-permute-start(s32[1]{0:T(128)} %slice.30), channel_id=1, source_target_pairs={{0,4},{4,8},{8,12},{12,16},{16,20},{20,24},{24,28},{28,32},{32,36}... | collective-permute-start | bytes 20 | tf_op jit(solution)/shard_map/ppermute | solution.py:429
  87.6 1.6 copy-start
  87.6 1.6 copy-start.1
  89.9 1.9 slice-start
  152.9 1.3 copy-start.2
  152.9 148.8 %reduce-scatter.5.cloned.1.call-start = ((), (), s32[]{:S(2)}) async-start(), calls=%async_computation.3 | async-start | bytes 5242880 | tf_op jit(solution)/shard_map/reduce_scatter | solution.py:448
Sparse Core Ops, SparseCore 0:
  10.8 63.9 all-gather.1
  153.0 97.9 reduce-scatter.6
  254.0 47.6 reduce-scatter.4
where the time goes:
time: 309 us; the launch traced here: 308 us
  waiting for transfers between devices  171 us (55%)
  Pallas kernels  45.9 us (15%)
  matrix products  35.7 us (12%)
  local copies, waits for them, and re-layouts  32.1 us (10%)
  between operations  13.8 us (4%)
  starting transfers between devices  5.04 us (2%)
  other arithmetic  4.47 us (1%)
    unnamed x4, waiting for transfers between devices  71.1 us
    all_gather x1, waiting for transfers between devices, body(): w_all = lax.all_gather(w_local, 'seq', axis=0, tiled=True)  54 us
    reduce_scatter x1, waiting for transfers between devices, body(): lax.psum_scatter(hidden_terms.astype(BF16), 'head', scatter_dimension=1,...  46.1 us
    pallas_call x1, Pallas kernels, scan_call(): pl.pallas_call(functools.partial(scan_kernel, n), name='scan', out_shape=...  34.1 us
    unnamed x10, local copies, waits for them, and re-layouts  19.7 us
    dot_general x1, matrix products, body(): projected = jnp.dot(hidden, w_all, preferred_element_type=F32)  12.8 us
    dot_general x1, matrix products, body(): lax.dot_general(grad_cols, w_all, (((1,), (1,)), ((), ())), preferred_ele...  12.5 us
    pallas_call x1, Pallas kernels, total_call(): pl.pallas_call(functools.partial(total_kernel, n), name='total', out_shap...  11.8 us
  transfers between devices with their start and end apart: 4, of which 3 were waited for; matrix products, arithmetic and copies ran while one was open for 8% of the time, Pallas kernels for 4%

commit v1 on v0

--- a/solution.py
+++ b/solution.py
@@ -60,8 +60,7 @@
 
 def scan_kernel(
     n,
-    xp_ref,
-    bc_ref,
+    pr_ref,
     dtp_ref,
     gap_ref,
     rate_ref,
@@ -93,7 +92,8 @@
     send2,
     recv2,
 ):
-    tokens, width = xp_ref.shape
+    tokens = pr_ref.shape[0]
+    width = pr_ref.shape[1] - 2 * STATE
     heads = dtp_ref.shape[0]
     blocks = tokens // TILE
     piece = width // n
@@ -133,7 +133,7 @@
     sums_skip = jnp.zeros((heads, 1), F32)
     for b in range(blocks):
         rows = pl.ds(b * TILE, TILE)
-        xp = xp_ref[rows, :]
+        xp = pr_ref[rows, :width]
         xs = xp * sigmoid(xp)
         xs_ref[rows, :] = xs
         xd = xs * dtx_ref[rows, :]
@@ -142,8 +142,8 @@
         g = g_ref[rows, :].astype(F32)
         ge_ref[rows, :] = (g * spread(ecum[:, b * TILE : (b + 1) * TILE], pick)).astype(BF16)
         sums_skip += jnp.sum(gather_heads(pick, g * xs), axis=1, keepdims=True)
-    b_low = bc_ref[:, :STATE].astype(BF16)
-    c_low = bc_ref[:, STATE:].astype(BF16)
+    b_low = pr_ref[:, width : width + STATE].astype(BF16)
+    c_low = pr_ref[:, width + STATE :].astype(BF16)
 
     parts = split3(jnp.broadcast_to(whole, (heads, STATE)))
     for k in range(3):
@@ -286,7 +286,7 @@
         r_parts.append(gather_heads(pick, xs * tq))
         off_parts.append(gather_heads(pick, ge_ref[rows, :].astype(F32) * dot(cc, s_in, NT)))
         grad_x = dtx_ref[rows, :] * z + skipx * g_ref[rows, :].astype(F32)
-        xp = xp_ref[rows, :]
+        xp = pr_ref[rows, :width]
         sig = sigmoid(xp)
         gcols_ref[rows, :width] = (grad_x * (sig + xp * sig * (1.0 - sig))).astype(BF16)
         grad_b = dot(xt_ref[rows, :], d_out, NN)
@@ -320,8 +320,8 @@
     sums_ref[...] = jnp.where(slot == 0, sum_a, jnp.where(slot == 1, sum_b, sums_skip))
 
 
-def scan_call(n, xp, bc, dtp, gap, rate, skip, g):
-    tokens, width = xp.shape
+def scan_call(n, proj, dtp, gap, rate, skip, g):
+    tokens, width = g.shape
     heads = dtp.shape[0]
     blocks = tokens // TILE
     piece = width // n
@@ -334,7 +334,7 @@
             jax.ShapeDtypeStruct((heads, tokens), BF16),
             jax.ShapeDtypeStruct((heads, 128), F32),
         ),
-        in_specs=[vm] * 7,
+        in_specs=[vm] * 6,
         out_specs=(vm, vm, vm),
         scratch_shapes=[
             pltpu.VMEM((n, 2 * piece + 16, STATE), BF16),
@@ -363,12 +363,306 @@
         compiler_params=pltpu.CompilerParams(
             collective_id=1, has_side_effects=True, vmem_limit_bytes=60 * 2**20
         ),
-    )(xp, bc, dtp, gap, rate, skip, g)
-
-
-def total_kernel(n, in_ref, out_ref, got, send, recv):
+    )(proj, dtp, gap, rate, skip, g)
+
+
+SIDE = 4
+
+
+def row_of(r):
+    return lax.rem(3 * (r + (r // 2) * (1 - 2 * lax.rem(r, 2))), SIDE)
+
+
+def place(n):
     me = lax.axis_index("seq")
+    core = lax.rem(me, 2)
+    chip = me // 2
+    y, z = chip // SIDE, lax.rem(chip, SIDE)
+    p = y * (1 - core) + z * core
+    q = z * (1 - core) + y * core
+
+    def chip_at(dp, dq):
+        return lax.rem(p + dp, SIDE) * (SIDE - (SIDE - 1) * core) + lax.rem(q + dq, SIDE) * (
+            1 + (SIDE - 1) * core
+        )
+
+    return me, core, chip_at
+
+
+def greet_all(barrier, ids):
+    for axis, to in ids:
+        pl.semaphore_signal(barrier, inc=1, device_id={axis: to}, device_id_type=MESH)
+
+
+def eye(size):
+    row = lax.broadcasted_iota(jnp.int32, (size, size), 0)
+    col = lax.broadcasted_iota(jnp.int32, (size, size), 1)
+    return jnp.where(row == col, 1.0, 0.0).astype(BF16)
+
+
+def gather_kernel(
+    n, cut, hid_hbm, wx_ref, wbc_ref, wdt_ref, bias_ref, proj_ref, dtp_ref, w_hbm, wall, hid, send, recv, local
+):
+    me, core, chip_at = place(n)
+    partner = me + 1 - 2 * core
+    inner, maps = wx_ref.shape[1], wbc_ref.shape[1]
+    wide = inner + maps
+    rows_all = wide + wdt_ref.shape[1]
+
+    def sid(dp, dq):
+        return 2 * chip_at(dp, dq) + core
+
     barrier = pltpu.get_barrier_semaphore()
+    to_p = (sid(1, 0), sid(3, 0))
+    to_q = (sid(0, 1), sid(0, 3))
+    greet_all(barrier, [("seq", d) for d in to_p + to_q + (partner,)])
+    load = pltpu.make_async_copy(hid_hbm, hid, local.at[n // 2])
+    load.start()
+    wall[me, :inner, :] = wx_ref[...].T
+    wall[me, inner:wide, :] = wbc_ref[...].T
+    wall[me, wide:, :] = dot(wdt_ref[...], eye(128), TN).astype(BF16)
+    halves = (pl.ds(0, cut), pl.ds(cut, rows_all - cut))
+    pl.semaphore_wait(barrier, 5)
+
+    def copy(slot, half, to, sem):
+        ref = wall.at[slot, halves[half]]
+        return pltpu.make_async_remote_copy(
+            ref, ref, send.at[sem], recv.at[2 * slot + half], {"seq": to}, MESH
+        )
+
+    sent = []
+
+    def push(slot, half, to):
+        c = copy(slot, half, to, len(sent))
+        c.start()
+        sent.append(c)
+
+    def arrive(slot, half):
+        copy(slot, half, partner, 0).wait_recv()
+
+    for half in range(2):
+        push(me, half, to_q[0])
+        push(me, 1 - half, to_q[1])
+        push(me, half, to_p[0])
+        push(me, 1 - half, to_p[1])
+    for half in range(2):
+        push(me, half, partner)
+
+    def along_q(slot, half):
+        push(slot, half, to_q[0])
+        push(slot, half, to_q[1])
+        push(slot, half, partner)
+
+    for dp, half, forward in ((3, 0, 0), (1, 1, 1), (3, 1, None), (1, 0, None)):
+        slot = sid(dp, 0)
+        arrive(slot, half)
+        if forward is not None:
+            push(slot, half, to_p[forward])
+        along_q(slot, half)
+
+    base = 30
+
+    def round_copies(r):
+        dp = row_of(r)
+        out = []
+        for i, (dq, half, forward) in enumerate(
+            ((3, 0, 0), (1, 1, 1), (3, 1, None), (1, 0, None), (2, 0, None), (2, 1, None))
+        ):
+            slot = sid(dp, dq)
+            some = []
+            if forward is not None:
+                some.append(copy(slot, half, to_q[forward], base + r * 8 + 6 + forward))
+            some.append(copy(slot, half, partner, base + r * 8 + i))
+            out.append((slot, half, some))
+        return out
+
+    def out_copy(chip):
+        return pltpu.make_async_copy(
+            wall.at[pl.ds(2 * chip, 2)], w_hbm.at[pl.ds(2 * chip, 2)], local.at[chip]
+        )
+
+    def take(chip):
+        other = 2 * chip + 1 - core
+        for half in range(2):
+            copy(other, half, partner, 0).wait_recv()
+        out_copy(chip).start()
+        a = hid[:, pl.ds(pl.multiple_of(chip * 256, 256), 256)]
+        b = jnp.concatenate([wall[2 * chip], wall[2 * chip + 1]], axis=1)
+        proj_ref[...] += dot(a, b[:wide], NT)
+        dtp_ref[...] += dot(b[wide:], a, NT)
+
+    def one_round(r, carry):
+        for slot, half, some in round_copies(r):
+            copy(slot, half, partner, 0).wait_recv()
+            for c in some:
+                c.start()
+
+        def chips(k, carry):
+            second = k // (r + 1)
+            a = r * (1 - second) + (k - r - 1) * second
+            b = k * (1 - second) + r * second
+            take(chip_at(row_of(a), row_of(b)))
+            return carry
+
+        lax.fori_loop(0, 2 * r + 1, chips, 0)
+        return carry
+
+    proj_ref[...] = jnp.zeros_like(proj_ref)
+    dtp_ref[...] = jnp.broadcast_to(bias_ref[...], dtp_ref.shape)
+    load.wait()
+    for half in range(2):
+        slot = sid(2, 0)
+        arrive(slot, half)
+        along_q(slot, half)
+    assert len(sent) == base
+    lax.fori_loop(0, SIDE, one_round, 0)
+
+    for c in sent:
+        c.wait_send()
+
+    def done(r, carry):
+        for _, _, some in round_copies(r):
+            for c in some:
+                c.wait_send()
+        return carry
+
+    lax.fori_loop(0, SIDE, done, 0)
+
+    def stored(k, carry):
+        out_copy(k).wait()
+        return carry
+
+    lax.fori_loop(0, n // 2, stored, 0)
+
+
+def gather_call(n, hidden, w_x, w_bc, w_dt, bias):
+    tokens = hidden.shape[0]
+    heads = w_dt.shape[1]
+    wide = w_x.shape[1] + w_bc.shape[1]
+    rows = wide + heads
+    vm = pl.BlockSpec(memory_space=pltpu.VMEM)
+    hbm = pl.BlockSpec(memory_space=pl.ANY)
+    return pl.pallas_call(
+        functools.partial(gather_kernel, n, wide // 2),
+        name="gather",
+        out_shape=(
+            jax.ShapeDtypeStruct((tokens, wide), F32),
+            jax.ShapeDtypeStruct((heads, tokens), F32),
+            jax.ShapeDtypeStruct((n, rows, 128), BF16),
+        ),
+        in_specs=[hbm, vm, vm, vm, vm],
+        out_specs=(vm, vm, hbm),
+        scratch_shapes=[
+            pltpu.VMEM((n, rows, 128), BF16),
+            pltpu.VMEM(hidden.shape, BF16),
+            pltpu.SemaphoreType.DMA((62,)),
+            pltpu.SemaphoreType.DMA((2 * n,)),
+            pltpu.SemaphoreType.DMA((n // 2 + 1,)),
+        ],
+        compiler_params=pltpu.CompilerParams(
+            collective_id=3, has_side_effects=True, vmem_limit_bytes=60 * 2**20
+        ),
+    )(hidden, w_x, w_bc, w_dt, bias)
+
+
+class Ring:
+    def __init__(self, axis, ids, cut, total, send, recv, base):
+        self.axis, self.ids, self.base = axis, ids, base
+        self.send, self.recv = send, recv
+        self.rows = (pl.ds(0, cut), pl.ds(cut, total - cut))
+
+    def bind(self, blocks, rel, fin):
+        self.blocks, self.rel, self.fin = blocks, rel, fin
+        low, high = self.rows
+        plan = (
+            (2, low, rel.at[low], 0),
+            (2, high, rel.at[high], 1),
+            (1, high, fin.at[0, high], 0),
+            (3, low, fin.at[1, low], 1),
+            (1, low, fin.at[0, low], 0),
+            (3, high, fin.at[1, high], 1),
+        )
+        self.copies = [
+            pltpu.make_async_remote_copy(
+                blocks[b].at[rows],
+                dst,
+                self.send.at[self.base + k],
+                self.recv.at[self.base + k],
+                {self.axis: self.ids[side]},
+                MESH,
+            )
+            for k, (b, rows, dst, side) in enumerate(plan)
+        ]
+        return self
+
+    def relay(self):
+        for k, (b, rows) in enumerate(((1, self.rows[0]), (3, self.rows[1]))):
+            self.copies[k].wait_recv()
+            ref = self.blocks[b]
+            ref[rows, :] = (ref[rows, :].astype(F32) + self.rel[rows, :].astype(F32)).astype(BF16)
+            self.copies[4 + k].start()
+
+    def final(self):
+        for k in range(2, 6):
+            self.copies[k].wait_recv()
+        own = self.blocks[0][...].astype(F32)
+        return own + self.fin[0].astype(F32) + self.fin[1].astype(F32)
+
+    def drain(self):
+        for c in self.copies:
+            c.wait_send()
+
+
+def scatter_kernel(
+    n,
+    cut,
+    hid_hbm,
+    w_hbm,
+    g_ref,
+    gdt_ref,
+    sums_ref,
+    dh_ref,
+    dwx_ref,
+    dwbc_ref,
+    dwdt_ref,
+    tot_ref,
+    hid,
+    w,
+    gt,
+    xbuf,
+    xrel,
+    xfin,
+    mine,
+    theirs,
+    fromp,
+    rel,
+    fin,
+    got,
+    send_p,
+    recv_p,
+    send_r,
+    recv_r,
+    send_s,
+    recv_s,
+    local,
+):
+    me, core, chip_at = place(n)
+    partner = me + 1 - 2 * core
+    head = lax.axis_index("head")
+    tokens, wide = g_ref.shape
+    inner = dwx_ref.shape[1]
+    rows_all = gt.shape[0]
+    per = n // SIDE
+    order = (2, 1, 3, 0)
+
+    def sid(dp, dq):
+        return 2 * chip_at(dp, dq) + core
+
+    def at_head(d):
+        return lax.rem(head + d, SIDE)
+
+    barrier = pltpu.get_barrier_semaphore()
+    x_ids = (at_head(1), at_head(3))
 
     def greet(k, carry):
         pl.semaphore_signal(
@@ -377,92 +671,236 @@
         return carry
 
     lax.fori_loop(1, n, greet, 0)
-    pl.semaphore_wait(barrier, n - 1)
-
-    def copy(k):
+    greet_all(barrier, [("head", d) for d in x_ids])
+
+    def w_copy(d):
+        part = pl.ds(at_head(d) * per, per)
+        return pltpu.make_async_copy(w_hbm.at[part], w.at[part], local.at[d])
+
+    w_copy(2).start()
+    load = pltpu.make_async_copy(hid_hbm, hid, local.at[SIDE])
+    load.start()
+    for d in (1, 3, 0):
+        w_copy(d).start()
+    gt[:wide, :] = g_ref[...].T
+    gt[wide:, :] = gdt_ref[...]
+
+    x_ring = Ring("head", x_ids, tokens // 2, tokens, send_r, recv_r, 0).bind(
+        [xbuf.at[d] for d in range(SIDE)], xrel, xfin
+    )
+    q_ids = (sid(0, 1), sid(0, 3))
+    p_ids = (sid(1, 0), sid(3, 0))
+    groups = {}
+    for g, a in enumerate(order):
+        groups[a] = Ring("seq", q_ids, cut, rows_all, send_r, recv_r, 6 + 6 * g).bind(
+            [mine.at[a * SIDE + b] for b in range(SIDE)], rel.at[g], fin.at[g]
+        )
+    p_ring = Ring("seq", p_ids, cut, rows_all, send_r, recv_r, 30).bind(
+        [mine.at[a * SIDE] for a in range(SIDE)], rel.at[SIDE], fin.at[SIDE]
+    )
+
+    def hidden_part(d):
+        first = at_head(d) * per
+
+        def one(k, carry):
+            b = jnp.concatenate([w[first + 2 * k], w[first + 2 * k + 1]], axis=1)
+            part = dot(g_ref[...], b[:wide], NN) + dot(gdt_ref[...], b[wide:], TN)
+            xbuf[d, :, pl.ds(pl.multiple_of(k * 256, 256), 256)] = part.astype(BF16)
+            return carry
+
+        lax.fori_loop(0, per // 2, one, 0)
+
+    def partner_copy(a, b):
+        return pltpu.make_async_remote_copy(
+            theirs.at[a * SIDE + b],
+            fromp.at[b * SIDE + a],
+            send_p.at[a * SIDE + b],
+            recv_p.at[b * SIDE + a],
+            {"seq": partner},
+            MESH,
+        )
+
+    def weight_part(a, b):
+        chip = chip_at(a, b)
+        at = a * SIDE + b
+        x = jnp.concatenate(
+            [
+                hid[:, pl.ds(pl.multiple_of(chip * 256 + 128 * core, 128), 128)],
+                hid[:, pl.ds(pl.multiple_of(chip * 256 + 128 * (1 - core), 128), 128)],
+            ],
+            axis=1,
+        )
+        part = dot(gt[...], x, NN).astype(BF16)
+        mine[at] = part[:, :128]
+        theirs[at] = part[:, 128:]
+        partner_copy(a, b).start()
+
+    def offset(r):
+        return row_of(SIDE - 1 - r)
+
+    def weight_ring(r):
+        left = SIDE - r
+
+        def one(k, carry):
+            second = k // left
+            a = r * (1 - second) + (k - left + r + 1) * second
+            b = (r + k) * (1 - second) + r * second
+            weight_part(offset(a), offset(b))
+            return carry
+
+        lax.fori_loop(0, 2 * left - 1, one, 0)
+
+    def pair_sums(r):
+        a = order[r]
+
+        def one(b, carry):
+            at = a * SIDE + b
+            partner_copy(b, a).wait_recv()
+            mine[at] = (mine[at].astype(F32) + fromp[at].astype(F32)).astype(BF16)
+            return carry
+
+        lax.fori_loop(0, SIDE, one, 0)
+        for k in range(4):
+            groups[a].copies[k].start()
+
+    def line_sum(r):
+        a = order[r]
+        mine[a * SIDE] = groups[a].final().astype(BF16)
+        if a == 2:
+            p_ring.copies[0].start()
+            p_ring.copies[1].start()
+        if a == 1:
+            p_ring.copies[2].start()
+        if a == 3:
+            p_ring.copies[3].start()
+
+    def sums_copy(k):
         to = lax.rem(me + k, n)
         return pltpu.make_async_remote_copy(
-            in_ref, got.at[me], send.at[k], recv.at[k], {"seq": to}, MESH
-        )
-
-    def start(k, carry):
-        copy(k).start()
-        return carry
-
-    lax.fori_loop(1, n, start, 0)
-    got[me] = in_ref[...]
-
-    def wait(k, carry):
-        copy(k).wait()
-        return carry
-
-    lax.fori_loop(1, n, wait, 0)
-    out_ref[...] = jnp.sum(got[...], axis=0)
-
-
-def total_call(n, value):
+            sums_ref, got.at[me], send_s.at[k], recv_s.at[k], {"seq": to}, MESH
+        )
+
+    w_copy(2).wait()
+    hidden_part(2)
+    pl.semaphore_wait(barrier, n + 1)
+    x_ring.copies[0].start()
+    x_ring.copies[1].start()
+    load.wait()
+    weight_ring(0)
+    pair_sums(0)
+    w_copy(1).wait()
+    w_copy(3).wait()
+    hidden_part(1)
+    x_ring.copies[2].start()
+    hidden_part(3)
+    x_ring.copies[3].start()
+    weight_ring(1)
+    pair_sums(1)
+    groups[2].relay()
+    weight_ring(2)
+    x_ring.relay()
+    pair_sums(2)
+    weight_ring(3)
+    groups[1].relay()
+    pair_sums(3)
+    line_sum(0)
+
+    def start_sums(k, carry):
+        sums_copy(k).start()
+        return carry
+
+    lax.fori_loop(1, n, start_sums, 0)
+    got[me] = sums_ref[...]
+    w_copy(0).wait()
+    hidden_part(0)
+    groups[3].relay()
+    line_sum(1)
+    groups[0].relay()
+    line_sum(2)
+    p_ring.relay()
+    line_sum(3)
+
+    def wait_sums(k, carry):
+        sums_copy(k).wait()
+        return carry
+
+    lax.fori_loop(1, n, wait_sums, 0)
+    tot_ref[...] = jnp.sum(got[...], axis=0)
+    grads = p_ring.final()
+    dwx_ref[...] = grads[:inner].T.astype(BF16)
+    dwbc_ref[...] = grads[inner:wide].T.astype(BF16)
+    dwdt_ref[...] = dot(grads[wide:].astype(BF16), eye(rows_all - wide), TN).astype(BF16)
+    dh_ref[...] = x_ring.final().astype(BF16)
+    x_ring.drain()
+    p_ring.drain()
+    for ring in groups.values():
+        ring.drain()
+
+    def drained(k, carry):
+        partner_copy(k // SIDE, lax.rem(k, SIDE)).wait_send()
+        return carry
+
+    lax.fori_loop(0, SIDE * SIDE, drained, 0)
+
+
+def scatter_call(n, hidden, w_all, gcols, gdt, sums):
+    tokens, wide = gcols.shape
+    heads = gdt.shape[0]
+    maps = 2 * STATE
+    inner = wide - maps
+    rows = wide + heads
+    per = hidden.shape[1] // SIDE
     vm = pl.BlockSpec(memory_space=pltpu.VMEM)
+    hbm = pl.BlockSpec(memory_space=pl.ANY)
+    chips = SIDE * SIDE
     return pl.pallas_call(
-        functools.partial(total_kernel, n),
-        name="total",
-        out_shape=jax.ShapeDtypeStruct(value.shape, value.dtype),
-        in_specs=[vm],
-        out_specs=vm,
+        functools.partial(scatter_kernel, n, wide // 2),
+        name="scatter",
+        out_shape=(
+            jax.ShapeDtypeStruct((tokens, per), BF16),
+            jax.ShapeDtypeStruct((128, inner), BF16),
+            jax.ShapeDtypeStruct((128, maps), BF16),
+            jax.ShapeDtypeStruct((128, heads), BF16),
+            jax.ShapeDtypeStruct(sums.shape, F32),
+        ),
+        in_specs=[hbm, hbm, vm, vm, vm],
+        out_specs=(vm,) * 5,
         scratch_shapes=[
-            pltpu.VMEM((n,) + value.shape, value.dtype),
+            pltpu.VMEM(hidden.shape, BF16),
+            pltpu.VMEM((n, rows, 128), BF16),
+            pltpu.VMEM((rows, tokens), BF16),
+            pltpu.VMEM((SIDE, tokens, per), BF16),
+            pltpu.VMEM((tokens, per), BF16),
+            pltpu.VMEM((2, tokens, per), BF16),
+            pltpu.VMEM((chips, rows, 128), BF16),
+            pltpu.VMEM((chips, rows, 128), BF16),
+            pltpu.VMEM((chips, rows, 128), BF16),
+            pltpu.VMEM((SIDE + 1, rows, 128), BF16),
+            pltpu.VMEM((SIDE + 1, 2, rows, 128), BF16),
+            pltpu.VMEM((n,) + sums.shape, F32),
+            pltpu.SemaphoreType.DMA((chips,)),
+            pltpu.SemaphoreType.DMA((chips,)),
+            pltpu.SemaphoreType.DMA((36,)),
+            pltpu.SemaphoreType.DMA((36,)),
             pltpu.SemaphoreType.DMA((n,)),
             pltpu.SemaphoreType.DMA((n,)),
+            pltpu.SemaphoreType.DMA((SIDE + 1,)),
         ],
-        compiler_params=pltpu.CompilerParams(collective_id=2, has_side_effects=True),
-    )(value)
+        compiler_params=pltpu.CompilerParams(
+            collective_id=4, has_side_effects=True, vmem_limit_bytes=62 * 2**20
+        ),
+    )(hidden, w_all, gcols, gdt, sums)
 
 
 def body(n, hidden, positions, w_x, w_bc, w_dt, a_log, dt_bias, d_skip, grad_out):
-    inner = w_x.shape[1]
-    heads = w_dt.shape[1]
-    maps = w_bc.shape[1]
-    w_local = jnp.concatenate([w_x, w_bc, w_dt], axis=1)
-    w_all = lax.all_gather(w_local, "seq", axis=0, tiled=True)
-    projected = jnp.dot(hidden, w_all, preferred_element_type=F32)
-    dtp = projected[:, inner + maps :].T + dt_bias[:, None]
     pairs = [(i, i + 1) for i in range(n - 1)]
     earlier = lax.ppermute(positions[-1:], "seq", pairs)
     gap = (positions - jnp.concatenate([earlier, positions[:-1]])).astype(F32)[None, :]
     rate = jnp.exp(a_log)[:, None]
-    gcols, gdt, sums = scan_call(
-        n,
-        projected[:, :inner],
-        projected[:, inner : inner + maps],
-        dtp,
-        gap,
-        rate,
-        d_skip[:, None],
-        grad_out,
-    )
-    totals = total_call(n, sums)
-    d_head_params = totals[:, :3].T
-    grad_cols = jnp.concatenate([gcols, gdt.T], axis=1)
-    hidden_terms = lax.dot_general(
-        grad_cols, w_all, (((1,), (1,)), ((), ())), preferred_element_type=F32
-    )
-    d_hidden = lax.psum_scatter(
-        hidden_terms.astype(BF16), "head", scatter_dimension=1, tiled=True
-    )
-    weight_grads = lax.psum_scatter(
-        lax.dot_general(
-            hidden, grad_cols, (((0,), (0,)), ((), ())), preferred_element_type=F32
-        ).astype(BF16),
-        "seq",
-        scatter_dimension=0,
-        tiled=True,
-    )
-    return (
-        d_hidden,
-        weight_grads[:, :inner],
-        weight_grads[:, inner : inner + maps],
-        weight_grads[:, inner + maps :],
-        d_head_params,
-    )
+    proj, dtp, w_all = gather_call(n, hidden, w_x, w_bc, w_dt, dt_bias[:, None])
+    gcols, gdt, sums = scan_call(n, proj, dtp, gap, rate, d_skip[:, None], grad_out)
+    d_hidden, d_w_x, d_w_bc, d_w_dt, totals = scatter_call(n, hidden, w_all, gcols, gdt, sums)
+    return d_hidden, d_w_x, d_w_bc, d_w_dt, totals[:, :3].T
 
 
 def solution(mesh):

time: 309 us -> 166 us (0.54)
  waiting for transfers between devices: 171 us -> 0.01 us
  Pallas kernels: 45.9 us -> 143 us
  matrix products: 35.7 us -> 0 us
  local copies, waits for them, and re-layouts: 32.1 us -> 14.9 us
  between operations: 13.8 us -> 0.69 us
  other arithmetic: 4.47 us -> 1.29 us
    pallas_call x1 -> x2, Pallas kernels: 11.8 us -> 110 us  [the longest x1 55.6 us: gather_call(): pl.pallas_call(functools.partial(gather_kernel, n, wide // 2), name='gath...]
    unnamed x4 -> x0, waiting for transfers between devices: 71.1 us -> none
    all_gather x1 -> x0, waiting for transfers between devices: 54 us -> none  [body(): w_all = lax.all_gather(w_local, 'seq', axis=0, tiled=True)]
    reduce_scatter x1 -> x0, waiting for transfers between devices: 46.1 us -> none  [body(): lax.psum_scatter(hidden_terms.astype(BF16), 'head', scatter_dimension=1,...]
    dot_general x3 -> x0, matrix products: 35.7 us -> none  [the longest x1 12.8 us: body(): projected = jnp.dot(hidden, w_all, preferred_element_type=F32)]
    unnamed x10 -> x8, local copies, waits for them, and re-layouts: 19.7 us -> 8.89 us
    slice x8 -> x0, local copies, waits for them, and re-layouts: 6.93 us -> none  [the longest x2 2.03 us: body(): projected[:, :inner]]
  transfers between devices with their start and end apart: 4 -> 1, of which waited for: 3 -> 0; matrix products, arithmetic and copies ran while one was open for 8% -> 3% of each run, Pallas kernels for 4% -> 34%
where the time goes in v1:
time: 166 us; the launch traced here: 165 us
  Pallas kernels  143 us (86%)
  local copies, waits for them, and re-layouts  14.9 us (9%)
  starting transfers between devices  4.91 us (3%)
    pallas_call x1, Pallas kernels, gather_call(): pl.pallas_call(functools.partial(gather_kernel, n, wide // 2), name='gath...  55.6 us
    pallas_call x1, Pallas kernels, scatter_call(): pl.pallas_call(functools.partial(scatter_kernel, n, wide // 2), name='sca...  54.3 us
    pallas_call x1, Pallas kernels, scan_call(): pl.pallas_call(functools.partial(scan_kernel, n), name='scan', out_shape=...  33.2 us
    unnamed x8, local copies, waits for them, and re-layouts  8.89 us
    ppermute x1, starting transfers between devices, body(): earlier = lax.ppermute(positions[-1:], 'seq', pairs)  4.91 us
  transfers between devices with their start and end apart: 1, of which 0 were waited for; matrix products, arithmetic and copies ran while one was open for 3% of the time, Pallas kernels for 34%

profile of v1, /device:TPU:1, one launch (start us, length us, event | category | flops | bytes accessed | tf_op | source)
XLA Modules:
  0.0 165.0 jit_solution(1912363877487620790)
XLA Ops:
  0.6 0.0 copy-start
  0.6 1.3 slice.9
  2.0 4.9 %collective-permute-start = (s32[1]{0:T(128)}, s32[1]{0:T(128)}, u32[]{:S(2)}, u32[]{:S(2)}) collective-permute-start(s32[1]{0:T(128)} %slice.9), channel_id=1, source_target_pairs={{0,4},{4,8},{8,12},{12,16},{16,20},{20,24},{24,28},{28,32},{32,36}... | collective-permute-start | bytes 20 | tf_op jit(solution)/shard_map/ppermute | solution.py:897
  6.9 0.7 exponential_bitcast_fusion
  7.6 0.7 copy.16.rate_ref
  8.2 1.3 copy.15.bias_ref
  9.6 1.3 copy.17.skip_ref
  10.9 1.4 copy.14.wdt_ref
  12.3 55.6 %gather.1 = (f32[512,1280]{1,0:T(8,128)}, f32[16,512]{1,0:T(8,128)}, bf16[32,1296,128]{2,1,0:T(8,128)(2,1)}) custom-call(bf16[512,4096]{1,0:T(8,128)(2,1)} %hid_hbm.3, bf16[128,1024]{1,0:T(8,128)(2,1)} %wx_ref.1, bf16[128,256]{1,0:T(8,128)(2,1)} %wbc_ref.1, bf16[128,16]{1,0:T(8,128)(2,1)} %copy.14.wdt_ref, f32[16,1]{1,0:T(8,128)} %copy.15.bias_ref), custom_call_target="tpu_custom_call" | custom-call | tf_op jit(solution)/shard_map/gather/pallas_call | solution.py:545
  67.9 0.0 collective-permute-done
  67.9 0.0 copy-done
  67.9 1.3 fusion
  69.2 33.2 %scan.1 = (bf16[512,1280]{1,0:T(8,128)(2,1)}, bf16[16,512]{1,0:T(8,128)(2,1)}, f32[16,128]{1,0:T(8,128)}) custom-call(f32[512,1280]{1,0:T(8,128)} %get-tuple-element.17.pr_ref, f32[16,512]{1,0:T(8,128)} %get-tuple-element.18.dtp_ref, f32[1,512]{1,0:T(1,128)} %bitcast.8, f32[16,1]{1,0:T(8,128)} %copy.16.rate_ref, f32[16,1]{1,0:T(8,128)} %copy.17.skip_ref, ...), custom_call_target="tpu_custom_call" | custom-call | tf_op jit(solution)/shard_map/scan/pallas_call | solution.py:329
  102.4 54.3 %scatter.1 = (bf16[512,1024]{1,0:T(8,128)(2,1)}, bf16[128,1024]{1,0:T(8,128)(2,1)}, bf16[128,256]{1,0:T(8,128)(2,1)}, bf16[128,16]{1,0:T(8,128)(2,1)}, f32[16,128]{1,0:T(8,128)}) custom-call(bf16[512,4096]{1,0:T(8,128)(2,1)} %hid_hbm.3, bf16[32,1296,128]{2,1,0:T(8,128)(2,1)} %get-tuple-element.16.w_hbm, bf16[512,1280]{1,0:T(8,128)(2,1)} %get-tuple-element.19.g_ref, ...), custom_call_target="tpu_custom_call" | custom-call | tf_op jit(solution)/shard_map/scatter/pallas_call | solution.py:856
  156.8 1.4 copy.18
  158.2 0.7 slice_bitcast_fusion
  158.9 0.7 copy.19
  159.6 2.3 %copy.23 = bf16[512,1024]{1,0:T(8,128)(2,1)} copy(bf16[512,1024]{1,0:T(8,128)(2,1)} %get-tuple-element.37) | data formatting | bytes 2097152
  161.8 1.7 %copy.24 = bf16[128,1024]{1,0:T(8,128)(2,1)} copy(bf16[128,1024]{1,0:T(8,128)(2,1)} %get-tuple-element.38) | data formatting | bytes 524288
  163.5 1.5 copy.25
Async XLA Ops:
  0.6 67.3 %copy-start = (s32[512]{0:T(512)S(1)}, s32[512]{0:T(512)}, u32[]{:S(2)}) copy-start(s32[512]{0:T(512)} %param.10) | copy-start | bytes 6148
  2.0 65.9 %collective-permute-start = (s32[1]{0:T(128)}, s32[1]{0:T(128)}, u32[]{:S(2)}, u32[]{:S(2)}) collective-permute-start(s32[1]{0:T(128)} %slice.9), channel_id=1, source_target_pairs={{0,4},{4,8},{8,12},{12,16},{16,20},{20,24},{24,28},{28,32},{32,36}... | collective-permute-start | bytes 20 | tf_op jit(solution)/shard_map/ppermute | solution.py:897

commit v2 on v1

--- a/solution.py
+++ b/solution.py
@@ -52,6 +52,12 @@
     row = lax.broadcasted_iota(jnp.int32, (heads, heads * width), 0)
     col = lax.broadcasted_iota(jnp.int32, (heads, heads * width), 1)
     return jnp.where(col // width == row, 1.0, 0.0).astype(BF16)
+
+
+def upright(row, size):
+    at = lax.broadcasted_iota(jnp.int32, (size, size), 0)
+    of = lax.broadcasted_iota(jnp.int32, (size, size), 1)
+    return jnp.sum(jnp.where(at == of, row, 0.0), axis=1, keepdims=True)
 
 
 def sigmoid(v):
@@ -74,6 +80,7 @@
     back,
     home,
     decs,
+    dgot,
     xs_ref,
     tail_ref,
     dtx_ref,
@@ -87,10 +94,13 @@
     dcbt_ref,
     rowe_ref,
     cole_ref,
+    gbc_ref,
     send1,
     recv1,
     send2,
     recv2,
+    send3,
+    recv3,
 ):
     tokens = pr_ref.shape[0]
     width = pr_ref.shape[1] - 2 * STATE
@@ -112,7 +122,7 @@
     pick = picker(heads, HEAD_DIM)
     dtp = dtp_ref[...]
     dt = jnp.maximum(dtp, 0.0) + jnp.log1p(jnp.exp(-jnp.abs(dtp)))
-    rate = rate_ref[...]
+    rate = jnp.exp(upright(rate_ref[...], heads))
     gap = gap_ref[...]
     decay = -rate * dt * gap
     before = lax.broadcasted_iota(jnp.int32, (tokens, tokens), 0)
@@ -127,43 +137,29 @@
     ecum = jnp.exp2(cum)
     tail = jnp.exp2(last - cum)
 
-    colb_ref[...] = spread(cum, picker(heads, 128))
-    dtx_ref[...] = spread(dt, pick)
-    tail_ref[...] = spread(tail, pick)
-    sums_skip = jnp.zeros((heads, 1), F32)
-    for b in range(blocks):
-        rows = pl.ds(b * TILE, TILE)
+    def prepare(b, carry):
+        rows = pl.ds(pl.multiple_of(b * TILE, TILE), TILE)
         xp = pr_ref[rows, :width]
         xs = xp * sigmoid(xp)
         xs_ref[rows, :] = xs
-        xd = xs * dtx_ref[rows, :]
-        xd_ref[rows, :] = xd.astype(BF16)
-        xt_ref[rows, :] = (xd * tail_ref[rows, :]).astype(BF16)
-        g = g_ref[rows, :].astype(F32)
-        ge_ref[rows, :] = (g * spread(ecum[:, b * TILE : (b + 1) * TILE], pick)).astype(BF16)
-        sums_skip += jnp.sum(gather_heads(pick, g * xs), axis=1, keepdims=True)
+        xt_ref[rows, :] = (xs * xd32_ref[rows, :]).astype(BF16)
+        ge_ref[rows, :] = (g_ref[rows, :].astype(F32) * u_ref[rows, :]).astype(BF16)
+        return carry
+
+    xd32_ref = tail_ref
+    xd32_ref[...] = spread(tail * dt, pick)
+    u_ref[...] = spread(ecum, pick)
+    lax.fori_loop(0, blocks, prepare, 0)
     b_low = pr_ref[:, width : width + STATE].astype(BF16)
     c_low = pr_ref[:, width + STATE :].astype(BF16)
-
-    parts = split3(jnp.broadcast_to(whole, (heads, STATE)))
-    for k in range(3):
-        decs[k] = parts[k].astype(F32)
+    decs[:, 0, :] = jnp.broadcast_to(whole, (heads, STATE))
     local_state = dot(xt_ref[...], b_low, TN).astype(BF16)
     local_adjoint = dot(ge_ref[...], c_low, TN).astype(BF16)
     pay[:, :piece, :] = local_state.reshape(n, piece, STATE)
-    pay[:, piece : 2 * piece, :] = local_adjoint.reshape(n, piece, STATE)
-    which = lax.broadcasted_iota(jnp.int32, (16, STATE), 0)
+    pay[:, piece:, :] = local_adjoint.reshape(n, piece, STATE)
     per_head = n // heads
-
-    def fill(h, carry):
-        one = [jnp.broadcast_to(decs[k, pl.ds(h, 1), :], (16, STATE)) for k in range(3)]
-        block = jnp.where(which == 0, one[0], jnp.where(which == 1, one[1], one[2])).astype(BF16)
-        for k in range(per_head):
-            pay[h * per_head + k, 2 * piece :, :] = block
-        return carry
-
-    lax.fori_loop(0, heads, fill, 0)
     got[me] = pay[me]
+    dgot[me] = decs[me // per_head]
     pl.semaphore_wait(barrier, n - 1)
 
     def out_copy(k):
@@ -172,12 +168,31 @@
             pay.at[to], got.at[me], send1.at[k], recv1.at[k], {"seq": to}, MESH
         )
 
+    def dec_copy(k):
+        to = lax.rem(me + k, n)
+        return pltpu.make_async_remote_copy(
+            decs.at[to // per_head], dgot.at[me], send3.at[k], recv3.at[k], {"seq": to}, MESH
+        )
+
     def start_out(k, carry):
         out_copy(k).start()
+        dec_copy(k).start()
         return carry
 
     lax.fori_loop(1, n, start_out, 0)
 
+    colb_ref[...] = spread(cum, picker(heads, 128))
+    dtx_ref[...] = spread(dt, pick)
+    tail_ref[...] = spread(tail, pick)
+
+    def prepare_more(b, total):
+        rows = pl.ds(pl.multiple_of(b * TILE, TILE), TILE)
+        xs = xs_ref[rows, :]
+        xd_ref[rows, :] = (xs * dtx_ref[rows, :]).astype(BF16)
+        dots = gather_heads(pick, g_ref[rows, :].astype(F32) * xs)
+        return total + jnp.sum(dots, axis=1, keepdims=True)
+
+    sums_skip = lax.fori_loop(0, blocks, prepare_more, jnp.zeros((heads, 1), F32))
     for i in range(blocks):
         for j in range(i, blocks):
             cbt_ref[i, j] = dot(
@@ -228,13 +243,13 @@
 
     def wait_out(k, carry):
         out_copy(k).wait_recv()
+        dec_copy(k).wait_recv()
         return carry
 
     lax.fori_loop(1, n, wait_out, 0)
 
     def decay_of(d):
-        rows = got[d, 2 * piece :, :].astype(F32)
-        return rows[0:1] + rows[1:2] + rows[2:3]
+        return dgot[d]
 
     def ahead(d, state):
         back[d, :piece, :] = state.astype(BF16)
@@ -243,7 +258,7 @@
     def behind(k, state):
         d = n - 1 - k
         back[d, piece:, :] = state.astype(BF16)
-        return decay_of(d) * state + got[d, piece : 2 * piece, :].astype(F32)
+        return decay_of(d) * state + got[d, piece:, :].astype(F32)
 
     zero = jnp.zeros((piece, STATE), F32)
     lax.fori_loop(0, n, ahead, zero)
@@ -263,19 +278,32 @@
     lax.fori_loop(1, n, start_back, 0)
     lax.fori_loop(pairs // 2, pairs, pair, 0)
 
+    for b in range(blocks):
+        rows = pl.ds(b * TILE, TILE)
+        grad_b = jnp.zeros((TILE, STATE), F32)
+        grad_c = jnp.zeros((TILE, STATE), F32)
+        for j in range(b, blocks):
+            grad_b += dot(dcbt_ref[b, j].astype(BF16), c_low[j * TILE : (j + 1) * TILE], NN)
+        for i in range(b + 1):
+            grad_c += dot(dcbt_ref[i, b].astype(BF16), b_low[i * TILE : (i + 1) * TILE], TN)
+        gbc_ref[rows, :STATE] = grad_b
+        gbc_ref[rows, STATE:] = grad_c
+    gcum = rowe_ref[...] - cole_ref[...].T[:heads]
+    skip = jnp.broadcast_to(upright(skip_ref[...], heads), (heads, 128))
+    skipx = spread(skip, pick)[0:1]
+
     def wait_back(k, carry):
         back_copy(k).wait_recv()
         back_copy(k).wait_send()
         out_copy(k).wait_send()
+        dec_copy(k).wait_send()
         return carry
 
     lax.fori_loop(1, n, wait_back, 0)
 
     s_in = home[:, :piece, :].reshape(width, STATE)
     d_out = home[:, piece:, :].reshape(width, STATE)
-    gcum = rowe_ref[...] - cole_ref[...].T[:heads]
     grad_dt_parts, r_parts, off_parts = [], [], []
-    skipx = spread(jnp.broadcast_to(skip_ref[...], (heads, 128)), pick)[0:1]
     for b in range(blocks):
         rows = pl.ds(b * TILE, TILE)
         bb, cc = b_low[b * TILE : (b + 1) * TILE], c_low[b * TILE : (b + 1) * TILE]
@@ -289,16 +317,8 @@
         xp = pr_ref[rows, :width]
         sig = sigmoid(xp)
         gcols_ref[rows, :width] = (grad_x * (sig + xp * sig * (1.0 - sig))).astype(BF16)
-        grad_b = dot(xt_ref[rows, :], d_out, NN)
-        grad_c = dot(ge_ref[rows, :], s_in, NN)
-        for j in range(b, blocks):
-            grad_b += dot(
-                dcbt_ref[b, j].astype(BF16), c_low[j * TILE : (j + 1) * TILE], NN
-            )
-        for i in range(b + 1):
-            grad_c += dot(
-                dcbt_ref[i, b].astype(BF16), b_low[i * TILE : (i + 1) * TILE], TN
-            )
+        grad_b = gbc_ref[rows, :STATE] + dot(xt_ref[rows, :], d_out, NN)
+        grad_c = gbc_ref[rows, STATE:] + dot(ge_ref[rows, :], s_in, NN)
         gcols_ref[rows, width : width + STATE] = grad_b.astype(BF16)
         gcols_ref[rows, width + STATE :] = grad_c.astype(BF16)
     grad_dt = jnp.concatenate(grad_dt_parts, axis=1)
@@ -337,11 +357,12 @@
         in_specs=[vm] * 6,
         out_specs=(vm, vm, vm),
         scratch_shapes=[
-            pltpu.VMEM((n, 2 * piece + 16, STATE), BF16),
-            pltpu.VMEM((n, 2 * piece + 16, STATE), BF16),
             pltpu.VMEM((n, 2 * piece, STATE), BF16),
             pltpu.VMEM((n, 2 * piece, STATE), BF16),
-            pltpu.VMEM((3, heads, STATE), F32),
+            pltpu.VMEM((n, 2 * piece, STATE), BF16),
+            pltpu.VMEM((n, 2 * piece, STATE), BF16),
+            pltpu.VMEM((heads, 1, STATE), F32),
+            pltpu.VMEM((n, 1, STATE), F32),
             pltpu.VMEM((tokens, width), F32),
             pltpu.VMEM((tokens, width), F32),
             pltpu.VMEM((tokens, width), F32),
@@ -355,6 +376,9 @@
             pltpu.VMEM((blocks, blocks, TILE, TILE), F32),
             pltpu.VMEM((heads, tokens), F32),
             pltpu.VMEM((tokens, 128), F32),
+            pltpu.VMEM((tokens, 2 * STATE), F32),
+            pltpu.SemaphoreType.DMA((n,)),
+            pltpu.SemaphoreType.DMA((n,)),
             pltpu.SemaphoreType.DMA((n,)),
             pltpu.SemaphoreType.DMA((n,)),
             pltpu.SemaphoreType.DMA((n,)),
@@ -369,10 +393,6 @@
 SIDE = 4
 
 
-def row_of(r):
-    return lax.rem(3 * (r + (r // 2) * (1 - 2 * lax.rem(r, 2))), SIDE)
-
-
 def place(n):
     me = lax.axis_index("seq")
     core = lax.rem(me, 2)
@@ -394,20 +414,33 @@
         pl.semaphore_signal(barrier, inc=1, device_id={axis: to}, device_id_type=MESH)
 
 
-def eye(size):
-    row = lax.broadcasted_iota(jnp.int32, (size, size), 0)
-    col = lax.broadcasted_iota(jnp.int32, (size, size), 1)
-    return jnp.where(row == col, 1.0, 0.0).astype(BF16)
-
-
 def gather_kernel(
-    n, cut, hid_hbm, wx_ref, wbc_ref, wdt_ref, bias_ref, proj_ref, dtp_ref, w_hbm, wall, hid, send, recv, local
+    n,
+    cut,
+    hid_hbm,
+    wx_ref,
+    wbc_ref,
+    wdt_ref,
+    bias_ref,
+    pos_ref,
+    proj_ref,
+    dtp_ref,
+    gap_ref,
+    w_hbm,
+    wall,
+    hid,
+    prev,
+    send,
+    recv,
+    local,
 ):
     me, core, chip_at = place(n)
     partner = me + 1 - 2 * core
     inner, maps = wx_ref.shape[1], wbc_ref.shape[1]
     wide = inner + maps
-    rows_all = wide + wdt_ref.shape[1]
+    heads = wdt_ref.shape[0]
+    rows_all = wide + heads
+    after = lax.rem(me + 1, n)
 
     def sid(dp, dq):
         return 2 * chip_at(dp, dq) + core
@@ -415,22 +448,23 @@
     barrier = pltpu.get_barrier_semaphore()
     to_p = (sid(1, 0), sid(3, 0))
     to_q = (sid(0, 1), sid(0, 3))
-    greet_all(barrier, [("seq", d) for d in to_p + to_q + (partner,)])
+    around = to_p + to_q + (partner, after, lax.rem(me + n - 1, n))
+    greet_all(barrier, [("seq", d) for d in around])
     load = pltpu.make_async_copy(hid_hbm, hid, local.at[n // 2])
     load.start()
     wall[me, :inner, :] = wx_ref[...].T
     wall[me, inner:wide, :] = wbc_ref[...].T
-    wall[me, wide:, :] = dot(wdt_ref[...], eye(128), TN).astype(BF16)
+    wall[me, wide:, :] = wdt_ref[...]
     halves = (pl.ds(0, cut), pl.ds(cut, rows_all - cut))
-    pl.semaphore_wait(barrier, 5)
+    pl.semaphore_wait(barrier, len(around))
+
+    sent = []
 
     def copy(slot, half, to, sem):
         ref = wall.at[slot, halves[half]]
         return pltpu.make_async_remote_copy(
             ref, ref, send.at[sem], recv.at[2 * slot + half], {"seq": to}, MESH
         )
-
-    sent = []
 
     def push(slot, half, to):
         c = copy(slot, half, to, len(sent))
@@ -447,87 +481,109 @@
         push(me, 1 - half, to_p[1])
     for half in range(2):
         push(me, half, partner)
-
-    def along_q(slot, half):
-        push(slot, half, to_q[0])
-        push(slot, half, to_q[1])
-        push(slot, half, partner)
-
-    for dp, half, forward in ((3, 0, 0), (1, 1, 1), (3, 1, None), (1, 0, None)):
+    place_copy = pltpu.make_async_remote_copy(
+        pos_ref, prev, local.at[n // 2 + 1], local.at[n // 2 + 2], {"seq": after}, MESH
+    )
+    place_copy.start()
+
+    def out_copy(chip):
+        return pltpu.make_async_copy(
+            wall.at[pl.ds(2 * chip, 2)], w_hbm.at[pl.ds(2 * chip, 2)], local.at[chip]
+        )
+
+    def take(dp, dq, first=False):
+        chip = chip_at(dp, dq)
+        other = 2 * chip + 1 - core
+        for half in range(2):
+            arrive(other, half)
+        out_copy(chip).start()
+        a = hid[:, pl.ds(pl.multiple_of(chip * 256, 256), 256)]
+        b = jnp.concatenate([wall[2 * chip], wall[2 * chip + 1]], axis=1)
+        x, t = dot(a, b[:wide], NT), dot(b[wide:], a, NT)
+        if first:
+            proj_ref[...] = x
+            dtp_ref[...] = t + upright(bias_ref[...], heads)
+        else:
+            proj_ref[...] += x
+            dtp_ref[...] += t
+
+    def takes(count, chip):
+        def one(k, carry):
+            take(*chip(k))
+            return carry
+
+        lax.fori_loop(0, count, one, 0)
+
+    def row_block(dp, half, forward=None):
         slot = sid(dp, 0)
         arrive(slot, half)
         if forward is not None:
             push(slot, half, to_p[forward])
-        along_q(slot, half)
-
-    base = 30
-
-    def round_copies(r):
-        dp = row_of(r)
-        out = []
-        for i, (dq, half, forward) in enumerate(
-            ((3, 0, 0), (1, 1, 1), (3, 1, None), (1, 0, None), (2, 0, None), (2, 1, None))
-        ):
+        push(slot, half, to_q[0])
+        push(slot, half, to_q[1])
+        push(slot, half, partner)
+
+    def onward(dp):
+        for side, dq in enumerate((3, 1)):
             slot = sid(dp, dq)
-            some = []
-            if forward is not None:
-                some.append(copy(slot, half, to_q[forward], base + r * 8 + 6 + forward))
-            some.append(copy(slot, half, partner, base + r * 8 + i))
-            out.append((slot, half, some))
-        return out
-
-    def out_copy(chip):
-        return pltpu.make_async_copy(
-            wall.at[pl.ds(2 * chip, 2)], w_hbm.at[pl.ds(2 * chip, 2)], local.at[chip]
-        )
-
-    def take(chip):
-        other = 2 * chip + 1 - core
+            arrive(slot, side)
+            push(slot, side, to_q[side])
+            push(slot, side, partner)
+
+    def rest(dp):
+        for side, dq in enumerate((3, 1)):
+            slot = sid(dp, dq)
+            arrive(slot, 1 - side)
+            push(slot, 1 - side, partner)
+
+    def opposite(dp):
         for half in range(2):
-            copy(other, half, partner, 0).wait_recv()
-        out_copy(chip).start()
-        a = hid[:, pl.ds(pl.multiple_of(chip * 256, 256), 256)]
-        b = jnp.concatenate([wall[2 * chip], wall[2 * chip + 1]], axis=1)
-        proj_ref[...] += dot(a, b[:wide], NT)
-        dtp_ref[...] += dot(b[wide:], a, NT)
-
-    def one_round(r, carry):
-        for slot, half, some in round_copies(r):
-            copy(slot, half, partner, 0).wait_recv()
-            for c in some:
-                c.start()
-
-        def chips(k, carry):
-            second = k // (r + 1)
-            a = r * (1 - second) + (k - r - 1) * second
-            b = k * (1 - second) + r * second
-            take(chip_at(row_of(a), row_of(b)))
-            return carry
-
-        lax.fori_loop(0, 2 * r + 1, chips, 0)
-        return carry
-
-    proj_ref[...] = jnp.zeros_like(proj_ref)
-    dtp_ref[...] = jnp.broadcast_to(bias_ref[...], dtp_ref.shape)
+            slot = sid(dp, 2)
+            arrive(slot, half)
+            push(slot, half, partner)
+
     load.wait()
-    for half in range(2):
-        slot = sid(2, 0)
-        arrive(slot, half)
-        along_q(slot, half)
-    assert len(sent) == base
-    lax.fori_loop(0, SIDE, one_round, 0)
-
+    take(0, 0, True)
+    row_block(3, 0, 0)
+    row_block(1, 1, 1)
+    onward(0)
+    row_block(3, 1)
+    row_block(1, 0)
+    rest(0)
+    takes(4, lambda k: ((1 - k // 2) * (1 + 2 * lax.rem(k, 2)), (k // 2) * (1 + 2 * lax.rem(k, 2))))
+    row_block(2, 0)
+    row_block(2, 1)
+    onward(3)
+    onward(1)
+    opposite(0)
+    takes(2, lambda k: (2 * k, 2 - 2 * k))
+    rest(3)
+    rest(1)
+    onward(2)
+    takes(4, lambda k: (1 + 2 * lax.rem(k, 2), 1 + 2 * (k // 2)))
+    rest(2)
+    opposite(3)
+    opposite(1)
+    takes(
+        4,
+        lambda k: (
+            2 * (1 - k // 2) + (1 + 2 * lax.rem(k, 2)) * (k // 2),
+            (1 + 2 * lax.rem(k, 2)) * (1 - k // 2) + 2 * (k // 2),
+        ),
+    )
+    opposite(2)
+    take(2, 2)
+
+    place_copy.wait()
+    tokens = pos_ref.shape[1]
+    here = jnp.broadcast_to(pos_ref[...].astype(F32), (8, tokens))
+    there = jnp.broadcast_to(prev[...].astype(F32), (8, tokens))
+    there = jnp.where(me == 0, 0.0, pltpu.roll(there, 1, 1))
+    lane = lax.broadcasted_iota(jnp.int32, (8, tokens), 1)
+    gap_ref[...] = (here - jnp.where(lane == 0, there, pltpu.roll(here, 1, 1)))[0:1]
     for c in sent:
         c.wait_send()
 
-    def done(r, carry):
-        for _, _, some in round_copies(r):
-            for c in some:
-                c.wait_send()
-        return carry
-
-    lax.fori_loop(0, SIDE, done, 0)
-
     def stored(k, carry):
         out_copy(k).wait()
         return carry
@@ -535,9 +591,9 @@
     lax.fori_loop(0, n // 2, stored, 0)
 
 
-def gather_call(n, hidden, w_x, w_bc, w_dt, bias):
+def gather_call(n, hidden, w_x, w_bc, w_dt, bias, positions):
     tokens = hidden.shape[0]
-    heads = w_dt.shape[1]
+    heads = w_dt.shape[0]
     wide = w_x.shape[1] + w_bc.shape[1]
     rows = wide + heads
     vm = pl.BlockSpec(memory_space=pltpu.VMEM)
@@ -548,21 +604,23 @@
         out_shape=(
             jax.ShapeDtypeStruct((tokens, wide), F32),
             jax.ShapeDtypeStruct((heads, tokens), F32),
+            jax.ShapeDtypeStruct((1, tokens), F32),
             jax.ShapeDtypeStruct((n, rows, 128), BF16),
         ),
-        in_specs=[hbm, vm, vm, vm, vm],
-        out_specs=(vm, vm, hbm),
+        in_specs=[hbm, vm, vm, vm, vm, vm],
+        out_specs=(vm, vm, vm, hbm),
         scratch_shapes=[
             pltpu.VMEM((n, rows, 128), BF16),
             pltpu.VMEM(hidden.shape, BF16),
+            pltpu.VMEM(positions.shape, positions.dtype),
             pltpu.SemaphoreType.DMA((62,)),
             pltpu.SemaphoreType.DMA((2 * n,)),
-            pltpu.SemaphoreType.DMA((n // 2 + 1,)),
+            pltpu.SemaphoreType.DMA((n // 2 + 3,)),
         ],
         compiler_params=pltpu.CompilerParams(
             collective_id=3, has_side_effects=True, vmem_limit_bytes=60 * 2**20
         ),
-    )(hidden, w_x, w_bc, w_dt, bias)
+    )(hidden, w_x, w_bc, w_dt, bias, positions)
 
 
 class Ring:
@@ -653,7 +711,6 @@
     inner = dwx_ref.shape[1]
     rows_all = gt.shape[0]
     per = n // SIDE
-    order = (2, 1, 3, 0)
 
     def sid(dp, dq):
         return 2 * chip_at(dp, dq) + core
@@ -691,9 +748,9 @@
     q_ids = (sid(0, 1), sid(0, 3))
     p_ids = (sid(1, 0), sid(3, 0))
     groups = {}
-    for g, a in enumerate(order):
-        groups[a] = Ring("seq", q_ids, cut, rows_all, send_r, recv_r, 6 + 6 * g).bind(
-            [mine.at[a * SIDE + b] for b in range(SIDE)], rel.at[g], fin.at[g]
+    for a in range(SIDE):
+        groups[a] = Ring("seq", q_ids, cut, rows_all, send_r, recv_r, 6 + 6 * a).bind(
+            [mine.at[a * SIDE + b] for b in range(SIDE)], rel.at[a], fin.at[a]
         )
     p_ring = Ring("seq", p_ids, cut, rows_all, send_r, recv_r, 30).bind(
         [mine.at[a * SIDE] for a in range(SIDE)], rel.at[SIDE], fin.at[SIDE]
@@ -735,44 +792,29 @@
         theirs[at] = part[:, 128:]
         partner_copy(a, b).start()
 
-    def offset(r):
-        return row_of(SIDE - 1 - r)
-
-    def weight_ring(r):
-        left = SIDE - r
-
+    def weights(count, chip):
         def one(k, carry):
-            second = k // left
-            a = r * (1 - second) + (k - left + r + 1) * second
-            b = (r + k) * (1 - second) + r * second
-            weight_part(offset(a), offset(b))
+            weight_part(*chip(k))
             return carry
 
-        lax.fori_loop(0, 2 * left - 1, one, 0)
-
-    def pair_sums(r):
-        a = order[r]
-
-        def one(b, carry):
+        lax.fori_loop(0, count, one, 0)
+
+    def pairs(a, first, step, count):
+        def one(k, carry):
+            b = first + k * step
             at = a * SIDE + b
             partner_copy(b, a).wait_recv()
             mine[at] = (mine[at].astype(F32) + fromp[at].astype(F32)).astype(BF16)
             return carry
 
-        lax.fori_loop(0, SIDE, one, 0)
-        for k in range(4):
-            groups[a].copies[k].start()
-
-    def line_sum(r):
-        a = order[r]
+        lax.fori_loop(0, count, one, 0)
+
+    def start(ring, *kinds):
+        for k in kinds:
+            ring.copies[k].start()
+
+    def line_sum(a):
         mine[a * SIDE] = groups[a].final().astype(BF16)
-        if a == 2:
-            p_ring.copies[0].start()
-            p_ring.copies[1].start()
-        if a == 1:
-            p_ring.copies[2].start()
-        if a == 3:
-            p_ring.copies[3].start()
 
     def sums_copy(k):
         to = lax.rem(me + k, n)
@@ -780,30 +822,62 @@
             sums_ref, got.at[me], send_s.at[k], recv_s.at[k], {"seq": to}, MESH
         )
 
+    def near(k):
+        return 1 + 2 * lax.rem(k, 2)
+
     w_copy(2).wait()
     hidden_part(2)
     pl.semaphore_wait(barrier, n + 1)
-    x_ring.copies[0].start()
-    x_ring.copies[1].start()
+    start(x_ring, 0, 1)
     load.wait()
-    weight_ring(0)
-    pair_sums(0)
+    weight_part(2, 2)
+    weight_part(1, 2)
+    weight_part(2, 1)
+    pairs(2, 2, 1, 1)
+    start(groups[2], 0, 1)
+    pairs(1, 2, 1, 1)
+    start(groups[1], 0, 1)
+    weight_part(3, 2)
+    weight_part(2, 3)
+    pairs(3, 2, 1, 1)
+    start(groups[3], 0, 1)
+    pairs(2, 1, 2, 2)
+    start(groups[2], 2, 3)
+    weights(4, lambda k: (near(k), near(k // 2)))
+    groups[2].relay()
+    pairs(1, 1, 2, 2)
+    start(groups[1], 2, 3)
+    pairs(3, 1, 2, 2)
+    start(groups[3], 2, 3)
     w_copy(1).wait()
     w_copy(3).wait()
     hidden_part(1)
-    x_ring.copies[2].start()
+    start(x_ring, 2)
     hidden_part(3)
-    x_ring.copies[3].start()
-    weight_ring(1)
-    pair_sums(1)
-    groups[2].relay()
-    weight_ring(2)
+    start(x_ring, 3)
+    weights(2, lambda k: (2 * k, 2 - 2 * k))
+    groups[1].relay()
+    groups[3].relay()
+    pairs(0, 2, 1, 1)
+    start(groups[0], 0, 1)
+    weights(4, lambda k: (near(k) * (k // 2), near(k) * (1 - k // 2)))
     x_ring.relay()
-    pair_sums(2)
-    weight_ring(3)
-    groups[1].relay()
-    pair_sums(3)
-    line_sum(0)
+    pairs(0, 1, 2, 2)
+    start(groups[0], 2, 3)
+    pairs(2, 0, 1, 1)
+    line_sum(2)
+    start(p_ring, 0, 1)
+    groups[0].relay()
+    weight_part(0, 0)
+    w_copy(0).wait()
+    hidden_part(0)
+    pairs(1, 0, 1, 1)
+    line_sum(1)
+    start(p_ring, 2)
+    pairs(3, 0, 1, 1)
+    line_sum(3)
+    start(p_ring, 3)
+    p_ring.relay()
 
     def start_sums(k, carry):
         sums_copy(k).start()
@@ -811,25 +885,19 @@
 
     lax.fori_loop(1, n, start_sums, 0)
     got[me] = sums_ref[...]
-    w_copy(0).wait()
-    hidden_part(0)
-    groups[3].relay()
-    line_sum(1)
-    groups[0].relay()
-    line_sum(2)
-    p_ring.relay()
-    line_sum(3)
+    pairs(0, 0, 1, 1)
+    line_sum(0)
 
     def wait_sums(k, carry):
         sums_copy(k).wait()
         return carry
 
     lax.fori_loop(1, n, wait_sums, 0)
-    tot_ref[...] = jnp.sum(got[...], axis=0)
+    tot_ref[...] = jnp.sum(got[...], axis=0).T[:3]
     grads = p_ring.final()
     dwx_ref[...] = grads[:inner].T.astype(BF16)
     dwbc_ref[...] = grads[inner:wide].T.astype(BF16)
-    dwdt_ref[...] = dot(grads[wide:].astype(BF16), eye(rows_all - wide), TN).astype(BF16)
+    dwdt_ref[...] = grads[wide:].astype(BF16)
     dh_ref[...] = x_ring.final().astype(BF16)
     x_ring.drain()
     p_ring.drain()
@@ -860,8 +928,8 @@
             jax.ShapeDtypeStruct((tokens, per), BF16),
             jax.ShapeDtypeStruct((128, inner), BF16),
             jax.ShapeDtypeStruct((128, maps), BF16),
-            jax.ShapeDtypeStruct((128, heads), BF16),
-            jax.ShapeDtypeStruct(sums.shape, F32),
+            jax.ShapeDtypeStruct((heads, 128), BF16),
+            jax.ShapeDtypeStruct((3, heads), F32),
         ),
         in_specs=[hbm, hbm, vm, vm, vm],
         out_specs=(vm,) * 5,
@@ -892,15 +960,34 @@
     )(hidden, w_all, gcols, gdt, sums)
 
 
+def finish_kernel(*refs):
+    half = len(refs) // 2
+    for source, result in zip(refs[:half], refs[half:]):
+        result[...] = source[...]
+
+
+def finish_call(*values):
+    vm = pl.BlockSpec(memory_space=pltpu.VMEM)
+    return pl.pallas_call(
+        finish_kernel,
+        name="finish",
+        out_shape=tuple(jax.ShapeDtypeStruct(v.shape, v.dtype) for v in values),
+        in_specs=[vm] * len(values),
+        out_specs=(vm,) * len(values),
+    )(*values)
+
+
 def body(n, hidden, positions, w_x, w_bc, w_dt, a_log, dt_bias, d_skip, grad_out):
-    pairs = [(i, i + 1) for i in range(n - 1)]
-    earlier = lax.ppermute(positions[-1:], "seq", pairs)
-    gap = (positions - jnp.concatenate([earlier, positions[:-1]])).astype(F32)[None, :]
-    rate = jnp.exp(a_log)[:, None]
-    proj, dtp, w_all = gather_call(n, hidden, w_x, w_bc, w_dt, dt_bias[:, None])
-    gcols, gdt, sums = scan_call(n, proj, dtp, gap, rate, d_skip[:, None], grad_out)
-    d_hidden, d_w_x, d_w_bc, d_w_dt, totals = scatter_call(n, hidden, w_all, gcols, gdt, sums)
-    return d_hidden, d_w_x, d_w_bc, d_w_dt, totals[:, :3].T
+    proj, dtp, gap, w_all = gather_call(
+        n, hidden, w_x, w_bc, w_dt.T, dt_bias[None, :], positions[None, :]
+    )
+    gcols, gdt, sums = scan_call(
+        n, proj, dtp, gap, a_log[None, :], d_skip[None, :], grad_out
+    )
+    d_hidden, d_w_x, d_w_bc, d_w_dt, d_params = finish_call(
+        *scatter_call(n, hidden, w_all, gcols, gdt, sums)
+    )
+    return d_hidden, d_w_x, d_w_bc, d_w_dt.T, d_params
 
 
 def solution(mesh):

time: 166 us -> 128 us (0.77)
  Pallas kernels: 143 us -> 127 us
  local copies, waits for them, and re-layouts: 14.9 us -> 0 us
  starting transfers between devices: 4.91 us -> 0 us
    pallas_call x1, Pallas kernels: 55.6 us -> 44.2 us  [gather_call(): pl.pallas_call(functools.partial(gather_kernel, n, wide // 2), name='gath...]
    unnamed x8 -> x0, local copies, waits for them, and re-layouts: 8.89 us -> none
    ppermute x1 -> x0, starting transfers between devices: 4.91 us -> none  [body(): earlier = lax.ppermute(positions[-1:], 'seq', pairs)]
    pallas_call x1, Pallas kernels: 54.3 us -> 49.6 us  [scatter_call(): pl.pallas_call(functools.partial(scatter_kernel, n, wide // 2), name='sca...]
    broadcast_in_dim x4 -> x0, local copies, waits for them, and re-layouts: 4 us -> none  [the longest x2 1.35 us: body(): rate = jnp.exp(a_log)[:, None]]
    pallas_call x1, Pallas kernels: 33.2 us -> 30.7 us  [scan_call(): pl.pallas_call(functools.partial(scan_kernel, n), name='scan', out_shape=...]
    pallas_call x0 -> x1, Pallas kernels: none -> 2.41 us  [finish_call(): pl.pallas_call(finish_kernel, name='finish', out_shape=tuple((jax.ShapeDt...]
  transfers between devices with their start and end apart: 1 -> 0, of which waited for: 0 -> 0; matrix products, arithmetic and copies ran while one was open for 3% -> 0% of each run, Pallas kernels for 34% -> 0%
where the time goes in v2:
time: 128 us
  Pallas kernels  127 us (99%)
    pallas_call x1, Pallas kernels, scatter_call(): pl.pallas_call(functools.partial(scatter_kernel, n, wide // 2), name='sca...  49.6 us
    pallas_call x1, Pallas kernels, gather_call(): pl.pallas_call(functools.partial(gather_kernel, n, wide // 2), name='gath...  44.2 us
    pallas_call x1, Pallas kernels, scan_call(): pl.pallas_call(functools.partial(scan_kernel, n), name='scan', out_shape=...  30.7 us

profile of v2, /device:TPU:1, one launch (start us, length us, event | category | flops | bytes accessed | tf_op | source)
XLA Modules:
  0.0 127.6 jit_solution(15773530069032836171)
XLA Ops:
  0.6 44.2 %gather.1 = (f32[512,1280]{1,0:T(8,128)}, f32[16,512]{1,0:T(8,128)}, f32[1,512]{1,0:T(1,128)}, bf16[32,1296,128]{2,1,0:T(8,128)(2,1)}) custom-call(bf16[512,4096]{1,0:T(8,128)(2,1)} %hid_hbm.3, bf16[128,1024]{1,0:T(8,128)(2,1)} %wx_ref.1, bf16[128,256]{1,0:T(8,128)(2,1)} %wbc_ref.1, bf16[16,128]{1,0:T(8,128)(2,1)} %bitcast.6, f32[1,16]{1,0:T(1,128)} %bitcast.8, ...), custom_call_target="tpu_custom_call" | custom-call | tf_op jit(solution)/shard_map/gather/pallas_call | solution.py:601
  44.8 30.7 %scan.1 = (bf16[512,1280]{1,0:T(8,128)(2,1)}, bf16[16,512]{1,0:T(8,128)(2,1)}, f32[16,128]{1,0:T(8,128)}) custom-call(f32[512,1280]{1,0:T(8,128)} %get-tuple-element.23.pr_ref, f32[16,512]{1,0:T(8,128)} %get-tuple-element.24.dtp_ref, f32[1,512]{1,0:T(1,128)} %get-tuple-element.25.gap_ref, f32[1,16]{1,0:T(1,128)} %bitcast.9, f32[1,16]{1,0:T(1,128)} %bitcast.10, ...), custom_call_target="tpu_custom_call" | custom-call | tf_op jit(solution)/shard_map/scan/pallas_call | solution.py:349
  75.6 49.6 %scatter.1 = (bf16[512,1024]{1,0:T(8,128)(2,1)}, bf16[128,1024]{1,0:T(8,128)(2,1)}, bf16[128,256]{1,0:T(8,128)(2,1)}, bf16[16,128]{1,0:T(8,128)(2,1)}, f32[3,16]{1,0:T(4,128)}) custom-call(bf16[512,4096]{1,0:T(8,128)(2,1)} %hid_hbm.3, bf16[32,1296,128]{2,1,0:T(8,128)(2,1)} %get-tuple-element.22.w_hbm, bf16[512,1280]{1,0:T(8,128)(2,1)} %get-tuple-element.26.g_ref, ...), custom_call_target="tpu_custom_call" | custom-call | tf_op jit(solution)/shard_map/scatter/pallas_call | solution.py:924
  125.2 2.4 %finish.1 = (bf16[512,1024]{1,0:T(8,128)(2,1)}, bf16[128,1024]{1,0:T(8,128)(2,1)}, bf16[128,256]{1,0:T(8,128)(2,1)}, bf16[16,128]{1,0:T(8,128)(2,1)}, f32[3,16]{1,0:T(4,128)}) custom-call(bf16[512,1024]{1,0:T(8,128)(2,1)} %get-tuple-element.29.refs_0_, bf16[128,1024]{1,0:T(8,128)(2,1)} %get-tuple-element.30.refs_1_, ...), custom_call_target="tpu_custom_call" | custom-call | tf_op jit(solution)/shard_map/finish/pallas_call | solution.py:971
